TPU v7x, 128 devices: a whole 4x4x4 slice. The times are simulated.
128 devices in a mesh: dp: 8 (over y, core), mp: 16 (over x, z).
Axes of the slice: x: 4, y: 4, z: 4, core: 2. Of those that a mesh axis runs over, the one named last changes fastest.
Arguments:
- tokens: bfloat16 [1024, 8192], P('dp', 'mp'), may hold values from -6 to 6
- grad_out: bfloat16 [1024, 8192], P('dp', 'mp'), may hold values from -6 to 6
- gate_weight: bfloat16 [1024, 128, 128], P('mp'), may hold values from -0.1875 to 0.1875
- up_weight: bfloat16 [1024, 128, 128], P('mp'), may hold values from -0.1875 to 0.1875
- down_weight: bfloat16 [1024, 128, 128], P('mp'), may hold values from -0.125 to 0.125
- gate_block_pairs: int32 [1024, 2], replicated, may hold values from 0 to 111, as said below
- up_blocks: int32 [1024, 2], replicated, may hold values from 0 to 111, as said below
- down_blocks: int32 [1024, 2], replicated, may hold values from 0 to 111, as said below
- column_order: int32 [112], replicated, may hold values from 0 to 111, as said below
Outputs:
- hidden_owned: bfloat16 [1024, 14336], P('dp', 'mp')
- output: bfloat16 [1024, 8192], P('dp', 'mp')
- input_grad: bfloat16 [1024, 8192], P('dp', 'mp')
- gate_grad: bfloat16 [1024, 128, 128], P('mp', 'dp')
- up_grad: bfloat16 [1024, 128, 128], P('mp', 'dp')
- down_grad: bfloat16 [1024, 128, 128], P('mp', 'dp')
Inputs may be any that keep to these rules, and one draw needn't show every extreme that they name: A permutation of the hidden column blocks; index j of mp owns the column blocks column_order[j * 7] to column_order[(j + 1) * 7 - 1]. `gate_block_pairs`: row k holds the row block (of 64) and column block (of 112) of gate block k; no block appears twice; block k = i * 64 + j * 4 + s with 0 <= s < 4 lies in a column block owned by index j; every column block holds at least one block. `up_blocks`: as gate_block_pairs, for the up blocks. `down_blocks`: row k holds the hidden block (of 112) and width block (of 64) of down block k; no block appears twice; block k = i * 64 + j * 4 + s with 0 <= s < 4 lies in a hidden block owned by index j; every hidden block holds at least one block.
All inputs are finite; a program needn't handle non-finite values.
Results may differ from a plain program's by a relative error of at most 0.024.
Values may be sent and summed in bfloat16 or wider, within the bound.
No kernel may reach another device: no remote copies, remote signals or barrier semaphores. Data moves between devices by JAX's collectives and lax.ppermute only.
A program may use at most 128 MiB of HBM per device.

v0:
```python
import functools

import jax
import jax.numpy as jnp
from jax import lax
from jax.experimental import pallas as pl
from jax.experimental.pallas import tpu as pltpu
from jax.sharding import Mesh, PartitionSpec as P

BS = 128
UNROLL = 4
MP = ("x", "z")
DP = ("y", "c")
BF = jnp.bfloat16
F32 = jnp.float32
SMEM = pl.BlockSpec(memory_space=pltpu.SMEM)
ANY = pl.BlockSpec(memory_space=pl.ANY)
VMEM = pl.BlockSpec(memory_space=pltpu.VMEM)


def dot(a, b):
    return lax.dot_general(a, b, (((1,), (0,)), ((), ())), preferred_element_type=F32)


def dot_t(a, b):
    return lax.dot_general(a, b, (((1,), (1,)), ((), ())), preferred_element_type=F32)


def start_all(pairs, sems, first):
    copies = [pltpu.make_async_copy(a, b, sems.at[first + i]) for i, (a, b) in enumerate(pairs)]
    for copy in copies:
        copy.start()
    return copies


def wait_all(copies):
    for copy in copies:
        copy.wait()


def piece_pairs(slots, pieces, whole):
    half = whole.shape[0] // 2
    at = lambda part, i: whole.at[(part,) + (slice(None),) * (len(whole.shape) - 4) + (slots[i],)]
    own = [(pieces[i], at(slice(None), i)) for i in range(2)]
    early = [(pieces[2 * i - 2], at(slice(half), i)) for i in range(2, 8)]
    late = [(pieces[2 * i - 1], at(slice(half, 2 * half), i)) for i in range(2, 8)]
    return own, early, late


def wide(ref, block, per):
    lane = pl.multiple_of((block & (per - 1)) * BS, BS)
    return ref[block >> (per.bit_length() - 1), :, pl.ds(lane, BS)]


def each_block(low, high, rows, cols, quota, projections, visit):
    def share(i, carry):
        for proj in projections:
            for b in range(quota):
                k = (i * 3 + proj) * quota + b
                visit((i, proj, b), k, rows[k], cols[k])
        return carry

    lax.fori_loop(low, high, share, 0, unroll=UNROLL)


def send_parts(acc, stage, outs, sems, first, per, by_near):
    ring, copies = len(outs), []
    for hop in list(range(1, ring)) + [0]:
        for turn in range(ring):
            near = hop * ring + turn if by_near else turn * ring + hop
            for q in range(per):
                stage[hop, turn, :, q * BS : (q + 1) * BS] = acc[near * per + q].astype(BF)
        copies += start_all([(stage.at[hop], outs[hop])], sems, first + hop)
    return copies


def owner_kernel(rows, hops, cols, slots, x_all, *refs, ring, per, quota, owned, count):
    pieces, refs = refs[:count], refs[count:]
    act_ref, own_ref, result = refs[:3]
    outs, refs = refs[3 : 3 + ring], refs[3 + ring :]
    tok, cot, flipped, whole, acc, out_acc, flipped_hidden, stage, out_stage, sems = refs
    shares, members = whole.shape[0] // (3 * quota), tok.shape[0]
    half, line = whole.shape[0] // 2, members // 4

    def quarters(which, ref):
        return [(x_all.at[i * line : (i + 1) * line, which], ref.at[i * line : (i + 1) * line]) for i in range(4)]

    own, early, late = piece_pairs(slots, pieces, whole)
    tok_copies = start_all(quarters(0, tok), sems, 0)
    early_copies = start_all(own + early + quarters(1, cot), sems, 4)
    late_copies = start_all(late, sems, 4 + len(early_copies))
    acc[...] = jnp.zeros_like(acc)
    out_acc[...] = jnp.zeros_like(out_acc)

    index = lambda d: lax.broadcasted_iota(jnp.int32, (BS, BS), d)
    unit = jnp.where(index(0) == index(1), 1.0, 0.0).astype(BF)

    def add(at, k, r, c):
        proj, w = at[1], whole[k].reshape(BS, BS)
        if proj == 0:
            x = tok[at[0], :, at[2] * BS : (at[2] + 1) * BS]
            flipped[at[0] * per + at[2]] = x.T
        if proj < 2:
            acc[proj, c] += dot(wide(tok, r, per), w)
        else:
            acc[proj, c] += dot_t(wide(cot, r, per), w)

    wait_all(tok_copies + early_copies)
    each_block(0, shares // 2, rows, cols, quota, range(3), add)
    wait_all(late_copies)
    each_block(shares // 2, shares, rows, cols, quota, range(3), add)

    for c in range(owned):
        gate, up, grad = acc[0, c], acc[1, c], acc[2, c]
        s = jax.nn.sigmoid(gate)
        silu = gate * s
        hidden = (silu * up).astype(BF)
        act_ref[0, c] = hidden
        own_ref[:, c * BS : (c + 1) * BS] = hidden
        act_ref[1, c] = (grad * up * s * (1.0 + gate * (1.0 - s))).astype(BF)
        act_ref[2, c] = (grad * silu).astype(BF)
        flipped_hidden[c] = dot_t(unit, hidden).astype(BF)

    def down(at, k, r, c):
        out_acc[r] += dot(act_ref[0, c], whole[k].reshape(BS, BS))

    each_block(0, shares, hops, cols, quota, (2,), down)
    first = 4 + len(early_copies) + len(late_copies)
    copies = send_parts(out_acc, out_stage, outs, sems, first, per, True)

    def outer(at, k, r, c):
        if at[1] < 2:
            g = dot(flipped[r], act_ref[1 + at[1], c])
        else:
            g = dot(flipped_hidden[c], wide(cot, r, per))
        stage[:, k] = g.astype(BF).reshape(stage.shape[0], -1, BS)

    for part in range(4):
        each_block(part * shares // 4, (part + 1) * shares // 4, rows, cols, quota, range(3), outer)
        at = pl.ds(part * half // 2, half // 2)
        copies += start_all(
            [(stage.at[:, at], result.at[:, at])],
            sems,
            first + ring + part,
        )
    wait_all(copies)


def parts_kernel(rows, cols, slots, act_ref, *refs, ring, per, quota, count, projections):
    pieces, outs = refs[:count], refs[count : count + ring]
    acc, whole, stage, sems = refs[count + ring :]
    shares = whole.shape[0]
    some = slice(projections[0], projections[-1] + 1)
    own, early, late = [
        [(piece.at[:, some], place) for piece, place in pairs]
        for pairs in piece_pairs(slots, pieces, whole)
    ]
    early_copies = start_all(own + early, sems, 0)
    late_copies = start_all(late, sems, len(early_copies))
    acc[...] = jnp.zeros_like(acc)

    def add(at, k, r, c):
        w = whole[at[0], at[1] - projections[0], at[2]].reshape(BS, BS)
        if at[1] < 2:
            acc[r] += dot_t(act_ref[1 + at[1], c], w)
        else:
            acc[r] += dot(act_ref[0, c], w)

    wait_all(early_copies)
    each_block(0, shares // 2, rows, cols, quota, projections, add)
    wait_all(late_copies)
    each_block(shares // 2, shares, rows, cols, quota, projections, add)

    wait_all(send_parts(acc, stage, outs, sems, count, per, projections[0] == 2))


def pair_kernel(a, b, out, sems):
    wait_all(start_all([(a, out.at[0]), (b, out.at[1])], sems, 0))


def shift(value, axis, hop):
    size = lax.axis_size(axis)
    return lax.ppermute(value, axis, [(i, (i + hop) % size) for i in range(size)])


def total(*terms):
    return sum(t.astype(F32) for t in terms)


def spread(mine):
    half = mine.shape[0] // 2
    parts = mine[:half], mine[half:]
    up, down = [None] * 2, [None] * 2
    up[0], down[1] = shift(parts[0], "y", 1), shift(parts[1], "y", -1)
    up[1], down[0] = shift(parts[1], "y", 1), shift(parts[0], "y", -1)
    far = [shift(up[0], "y", 1), shift(down[1], "y", -1)]
    swap = lambda value: shift(value, "c", 1)
    pieces = [mine, swap(mine)]
    for pair in (up, down, far):
        pieces += pair + [swap(v) for v in pair]
    return pieces


def collect(outs, grads):
    ring = len(outs)
    first = [[p[0]] + [shift(p[h], a, -h) for h in range(1, ring)] for p, a in ((outs, "x"), (grads, "z"))]
    done = []
    for terms, axis in zip(first, ("z", "x")):
        sums = [total(*[t[turn] for t in terms]) for turn in range(ring)]
        arrived = [shift(sums[turn].astype(BF), axis, -turn) for turn in range(1, ring)]
        done.append(total(sums[0], *arrived).astype(BF))
    return done


def body(
    tokens,
    grad_out,
    gate_weight,
    up_weight,
    down_weight,
    gate_block_pairs,
    up_blocks,
    down_blocks,
    column_order,
):
    n_mp, n_dp = lax.axis_size(MP), lax.axis_size(DP)
    member, shard = lax.axis_index(MP), lax.axis_index(DP)
    x, y, z, core = (lax.axis_index(a) for a in ("x", "y", "z", "c"))
    ring = lax.axis_size("x")
    held = gate_weight.shape[0]
    quota = held // n_mp
    slab = BS // n_dp
    per = tokens.shape[1] // BS
    n_rows = per * n_mp
    owned = column_order.shape[0] // n_mp
    count = 3 * held
    tok = tokens.shape[0]

    pair = pl.pallas_call(
        pair_kernel,
        out_shape=jax.ShapeDtypeStruct((2,) + tokens.shape, BF),
        in_specs=[ANY] * 2,
        out_specs=ANY,
        scratch_shapes=[pltpu.SemaphoreType.DMA((2,))],
        name="pair",
    )(tokens, grad_out)
    x_all = lax.all_gather(pair, MP, axis=0, tiled=False)

    slabs = jnp.stack(
        [
            lax.dynamic_slice_in_dim(w, shard * slab, slab, 1).reshape(n_mp, quota, slab, BS)
            for w in (gate_weight, up_weight, down_weight)
        ],
        axis=1,
    )
    mine = lax.all_to_all(slabs, MP, split_axis=0, concat_axis=0, tiled=True)
    weights = spread(mine.reshape(count, slab, BS))

    tables = jnp.stack([gate_block_pairs, up_blocks, down_blocks])
    tables = tables.reshape(3, n_mp, n_mp, quota, 2)
    tables = lax.dynamic_index_in_dim(tables, member, 2, keepdims=False).transpose(1, 0, 2, 3)
    is_down = (jnp.arange(3) == 2)[None, :, None]
    rows = jnp.where(is_down, tables[..., 1], tables[..., 0]).reshape(count)
    names = jnp.where(is_down, tables[..., 0], tables[..., 1]).reshape(count)
    near, far = (x + ring - rows // (per * ring)) % ring, (z + ring - rows // per % ring) % ring
    hops = (near * ring + far) * per + rows % per
    own_cols = lax.dynamic_slice_in_dim(column_order, member * owned, owned, 0)
    cols = jnp.sum(
        jnp.where(names[:, None] == own_cols[None, :], jnp.arange(owned, dtype=jnp.int32), 0),
        axis=1,
    )
    slots = jnp.stack(
        [(y + hop + ring) % ring * 2 + c for hop in (0, -1, 1, 2) for c in (core, 1 - core)]
    ).astype(jnp.int32)

    act_shape = (3, owned, tok, BS)
    x_shape = (n_mp, tok, per * BS)
    grad_shape = (n_dp, count, slab, BS)
    whole = pltpu.VMEM((count, n_dp, slab, BS), BF)
    sizes = dict(ring=ring, per=per, quota=quota, count=len(weights))

    part_shape = (ring, tok, per * BS)
    act, hidden_own, grads, *out_parts = pl.pallas_call(
        functools.partial(owner_kernel, owned=owned, **sizes),
        out_shape=[jax.ShapeDtypeStruct(act_shape, BF), jax.ShapeDtypeStruct((tok, owned * BS), BF)]
        + [jax.ShapeDtypeStruct(grad_shape, BF)]
        + [jax.ShapeDtypeStruct(part_shape, BF)] * ring,
        in_specs=[SMEM] * 4 + [ANY] * (1 + len(weights)),
        out_specs=[VMEM] * 2 + [ANY] * (1 + ring),
        scratch_shapes=[
            pltpu.VMEM(x_shape, BF),
            pltpu.VMEM(x_shape, BF),
            pltpu.VMEM((n_rows, BS, tok), BF),
            whole,
            pltpu.VMEM(act_shape, F32),
            pltpu.VMEM((n_rows, tok, BS), F32),
            pltpu.VMEM((owned, BS, tok), BF),
            pltpu.VMEM(grad_shape, BF),
            pltpu.VMEM((ring,) + part_shape, BF),
            pltpu.SemaphoreType.DMA((len(weights) + 12 + ring,)),
        ],
        name="owner",
    )(rows, hops, cols, slots, x_all, *weights)
    grads = lax.psum_scatter(grads, DP, scatter_dimension=0, tiled=True)

    by_share = [w.reshape(-1, 3, quota, slab, BS) for w in weights]

    def parts_of(projections):
        return pl.pallas_call(
            functools.partial(parts_kernel, projections=projections, **sizes),
            out_shape=[jax.ShapeDtypeStruct(part_shape, BF)] * ring,
            in_specs=[SMEM] * 3 + [VMEM] + [ANY] * len(weights),
            out_specs=[ANY] * ring,
            scratch_shapes=[
                pltpu.VMEM((n_rows, tok, BS), F32),
                pltpu.VMEM((n_mp, len(projections), quota, n_dp, slab, BS), BF),
                pltpu.VMEM((ring,) + part_shape, BF),
                pltpu.SemaphoreType.DMA((len(weights) + ring,)),
            ],
        )(hops, cols, slots, act, *by_share)

    in_parts = parts_of((0, 1))
    output, input_grad = collect(out_parts, in_parts)
    grads = grads.reshape(n_mp, 3, quota, slab, BS)
    grads = lax.all_to_all(grads, MP, split_axis=0, concat_axis=0, tiled=True)
    gate_grad, up_grad, down_grad = (grads[:, p].reshape(held, slab, BS) for p in range(3))
    return (hidden_own, output, input_grad, gate_grad, up_grad, down_grad)


def solution(mesh):
    mesh = Mesh(mesh.devices.reshape(4, 2, 4, 4), DP + MP)
    wide_spec, block_spec, grad_spec = P(DP, MP), P(MP, None, None), P(MP, DP, None)
    return jax.shard_map(
        body,
        mesh=mesh,
        in_specs=(wide_spec,) * 2 + (block_spec,) * 3 + (P(),) * 4,
        out_specs=(wide_spec,) * 3 + (grad_spec,) * 3,
        check_vma=False,
    )
```

profile of v0, /device:TPU:0, one launch (start us, length us, event | category | flops | bytes accessed | tf_op | source)
XLA Modules:
  0.0 164.3 jit_solution(10417832973863857805)
XLA Ops:
  7.2 9.1 %pair.1 = bf16[2,128,512]{2,1,0:T(8,128)(2,1)} custom-call(bf16[128,512]{1,0:T(8,128)(2,1)} %a.1, bf16[128,512]{1,0:T(8,128)(2,1)} %b.1), custom_call_target="tpu_custom_call" | custom-call | tf_op jit(solution)/shard_map/pair/pallas_call | solution.py:239
  17.7 24.7 %all_to_all.10.refs_0_ = bf16[16,3,4,16,128]{4,3,2,1,0:T(8,128)(2,1)S(1)} all-to-all(bf16[16,3,4,16,128]{4,3,2,1,0:T(8,128)(2,1)S(1)} %pad_maximum_fusion), channel_id=1, replica_groups=mesh['y'=4,'c'=2,'x'=4,'z'=4] {'x','z'}, dimensions={0} | all-to-all | bytes 1572864 | tf_op jit(solution)/shard_map/all_to_all | solution.py:256
  43.4 2.9 %collective-permute-start.5 = (bf16[96,16,128]{2,1,0:T(8,128)(2,1)S(1)}, bf16[96,16,128]{2,1,0:T(8,128)(2,1)S(1)}, u32[]{:S(2)}, u32[]{:S(2)}) collective-permute-start(bf16[96,16,128]{2,1,0:T(8,128)(2,1)S(1)} %bitcast.81), channel_id=1, source_target_pairs={{0,96},{32,0},{64,32},{96,64},{1,97},{33,1},{65,33},{97,65},{2,98}... | collective-permute-start | bytes 1179656 | tf_op jit(solution)/shard_map/ppermute | solution.py:183
  46.3 3.2 %collective-permute-start.6 = (bf16[96,16,128]{2,1,0:T(8,128)(2,1)}, bf16[96,16,128]{2,1,0:T(8,128)(2,1)}, u32[]{:S(2)}, u32[]{:S(2)}) collective-permute-start(bf16[96,16,128]{2,1,0:T(8,128)(2,1)} %bitcast.17), channel_id=1, source_target_pairs={{0,96},{32,0},{64,32},{96,64},{1,97},{33,1},{65,33},{97,65},{2,98}... | collective-permute-start | bytes 1179656 | tf_op jit(solution)/shard_map/ppermute | solution.py:183
  49.5 6.3 %collective-permute-done.5.refs_6_ = bf16[96,16,128]{2,1,0:T(8,128)(2,1)S(1)} collective-permute-done((bf16[96,16,128]{2,1,0:T(8,128)(2,1)S(1)}, bf16[96,16,128]{2,1,0:T(8,128)(2,1)S(1)}, u32[]{:S(2)}, u32[]{:S(2)}) %collective-permute-start.5) | collective-permute-done | bytes 393248 | tf_op jit(solution)/shard_map/ppermute | solution.py:183
  55.8 3.8 %collective-permute-done.1.refs_2_ = bf16[96,16,128]{2,1,0:T(8,128)(2,1)} collective-permute-done((bf16[96,16,128]{2,1,0:T(8,128)(2,1)S(1)}, bf16[96,16,128]{2,1,0:T(8,128)(2,1)}, u32[]{:S(2)}, u32[]{:S(2)}) %collective-permute-start.1) | collective-permute-done | bytes 393248 | tf_op jit(solution)/shard_map/ppermute | solution.py:183
  61.0 3.7 %collective-permute-start.10 = (bf16[96,16,128]{2,1,0:T(8,128)(2,1)}, bf16[96,16,128]{2,1,0:T(8,128)(2,1)}, u32[]{:S(2)}, u32[]{:S(2)}) collective-permute-start(bf16[96,16,128]{2,1,0:T(8,128)(2,1)} %collective-permute-done.6.refs_7_), channel_id=1, source_target_pairs={{0,96},{32,0},{64,32},{96,64},{1,97},{33,1},{65,33},{97,65},{2,98}... | collective-permute-start | bytes 1179656 | tf_op jit(solution)/shard_map/ppermute | solution.py:183
  70.8 2.0 %collective-permute-done.9.refs_10_ = bf16[96,16,128]{2,1,0:T(8,128)(2,1)} collective-permute-done((bf16[96,16,128]{2,1,0:T(8,128)(2,1)}, bf16[96,16,128]{2,1,0:T(8,128)(2,1)}, u32[]{:S(2)}, u32[]{:S(2)}) %collective-permute-start.9) | collective-permute-done | bytes 393248 | tf_op jit(solution)/shard_map/ppermute | solution.py:183
  76.1 14.2 %owner.1 = (bf16[3,7,128,128]{3,2,1,0:T(8,128)(2,1)}, bf16[128,896]{1,0:T(8,128)(2,1)}, bf16[8,192,16,128]{3,2,1,0:T(8,128)(2,1)}, bf16[4,128,512]{2,1,0:T(8,128...) custom-call(s32[192]{0:T(256)} %get-tuple-element.29.rows, ...), custom_call_target="tpu_custom_call" | custom-call | tf_op jit(solution)/shard_map/owner/pallas_call | solution.py:283
  90.3 1.9 %collective-permute-start.13 = (bf16[4,128,512]{2,1,0:T(8,128)(2,1)}, bf16[4,128,512]{2,1,0:T(8,128)(2,1)S(1)}, u32[]{:S(2)}, u32[]{:S(2)}) collective-permute-start(bf16[4,128,512]{2,1,0:T(8,128)(2,1)} %get-tuple-element.19), channel_id=1, source_target_pairs={{0,12},{4,0},{8,4},{12,8},{1,13},{5,1},{9,5},{13,9},{2,14},{6,2},{... | collective-permute-start | bytes 1572872 | tf_op jit(solution)/shard_map/ppermute | solution.py:183
  93.4 7.9 %shard_map.136 = (bf16[4,128,512]{2,1,0:T(8,128)(2,1)}, bf16[4,128,512]{2,1,0:T(8,128)(2,1)}, bf16[4,128,512]{2,1,0:T(8,128)(2,1)}, bf16[4,128,512]{2,1,0:T(8,128)(2,1)}) custom-call(s32[192]{0:T(256)} %get-tuple-element.28.hops.rows, s32[192]{0:T(256)} %select_reduce_fusion.cols, s32[8]{0:T(128)} %stack.54.slots, ...), custom_call_target="tpu_custom_call" | custom-call | tf_op jit(solution)/shard_map/pallas_call | solution.py:309
  101.2 1.7 %collective-permute-start.19 = (bf16[4,128,512]{2,1,0:T(8,128)(2,1)}, bf16[4,128,512]{2,1,0:T(8,128)(2,1)}, u32[]{:S(2)}, u32[]{:S(2)}) collective-permute-start(bf16[4,128,512]{2,1,0:T(8,128)(2,1)} %get-tuple-element.24), channel_id=1, source_target_pairs={{0,3},{1,0},{2,1},{3,2},{4,7},{5,4},{6,5},{7,6},{8,11},{9,8},{10,9... | collective-permute-start | bytes 1572872 | tf_op jit(solution)/shard_map/ppermute | solution.py:183
  103.8 11.8 %collective-permute-done.13 = bf16[4,128,512]{2,1,0:T(8,128)(2,1)S(1)} collective-permute-done((bf16[4,128,512]{2,1,0:T(8,128)(2,1)}, bf16[4,128,512]{2,1,0:T(8,128)(2,1)S(1)}, u32[]{:S(2)}, u32[]{:S(2)}) %collective-permute-start.13) | collective-permute-done | bytes 524320 | tf_op jit(solution)/shard_map/ppermute | solution.py:183
  115.6 3.4 %collective-permute-done.15 = bf16[4,128,512]{2,1,0:T(8,128)(2,1)} collective-permute-done((bf16[4,128,512]{2,1,0:T(8,128)(2,1)}, bf16[4,128,512]{2,1,0:T(8,128)(2,1)}, u32[]{:S(2)}, u32[]{:S(2)}) %collective-permute-start.15) | collective-permute-done | bytes 524320 | tf_op jit(solution)/shard_map/ppermute | solution.py:183
  119.0 2.1 %fusion.6 = (bf16[128,512]{1,0:T(8,128)(2,1)}, bf16[128,512]{1,0:T(8,128)(2,1)}, bf16[128,512]{1,0:T(8,128)(2,1)S(1)}) fusion(bf16[4,128,512]{2,1,0:T(8,128)(2,1)} %collective-permute-done.15, bf16[4,128,512]{2,1,0:T(8,128)(2,1)} %collective-permute-done.14, bf16[4,128,512]{2,1,0:T(8,128)(2,1)S(1)} %collective-permute-done.13, ...), kind=kLoop, calls=%fused_computation.17 | loop fusion | flops 1572864 | bytes 1966080 | tf_op jit(solution)/shard_map/add | solution.py:187
  121.3 1.8 %collective-permute-start.18 = (bf16[128,512]{1,0:T(8,128)(2,1)}, bf16[128,512]{1,0:T(8,128)(2,1)S(1)}, u32[]{:S(2)}, u32[]{:S(2)}) collective-permute-start(bf16[128,512]{1,0:T(8,128)(2,1)} %get-tuple-element.34), channel_id=1, source_target_pairs={{0,1},{1,2},{2,3},{3,0},{4,5},{5,6},{6,7},{7,4},{8,9},{9,10},{10,1... | collective-permute-start | bytes 393224 | tf_op jit(solution)/shard_map/ppermute | solution.py:183
  123.1 8.0 %reduce-scatter.2.cloned.1.call-done = bf16[1,192,16,128]{3,2,1,0:T(8,128)(2,1)} async-done(((bf16[8,192,16,128]{3,2,1,0:T(8,128)(2,1)}), bf16[1,192,16,128]{3,2,1,0:T(8,128)(2,1)}) %reduce-scatter.2.cloned.1.call-update) | async-done | bytes 786448 | tf_op jit(solution)/shard_map/reduce_scatter | solution.py:304
  131.2 6.9 %all-to-all-start.1 = ((bf16[16,3,4,16,128]{4,3,2,1,0:T(8,128)(2,1)}), bf16[16,3,4,16,128]{4,3,2,1,0:T(8,128)(2,1)S(1)}, u32[]{:S(2)}, u32[]{:S(2)}) async-start(bf16[16,3,4,16,128]{4,3,2,1,0:T(8,128)(2,1)} %bitcast.80), calls=%async_computation.2 | async-start | bytes 1572864 | tf_op jit(solution)/shard_map/all_to_all | solution.py:325
  138.1 3.5 %collective-permute-start.17 = (bf16[128,512]{1,0:T(8,128)(2,1)S(1)}, bf16[128,512]{1,0:T(8,128)(2,1)S(1)}, u32[]{:S(2)}, u32[]{:S(2)}) collective-permute-start(bf16[128,512]{1,0:T(8,128)(2,1)S(1)} %get-tuple-element.35), channel_id=1, source_target_pairs={{0,2},{1,3},{2,0},{3,1},{4,6},{5,7},{6,4},{7,5},{8,10},{9,11},{10,... | collective-permute-start | bytes 393224 | tf_op jit(solution)/shard_map/ppermute | solution.py:183
  143.2 2.7 %collective-permute-start.22 = (bf16[128,512]{1,0:T(8,128)(2,1)S(1)}, bf16[128,512]{1,0:T(8,128)(2,1)S(1)}, u32[]{:S(2)}, u32[]{:S(2)}) collective-permute-start(bf16[128,512]{1,0:T(8,128)(2,1)S(1)} %get-tuple-element.30), channel_id=1, source_target_pairs={{0,12},{4,0},{8,4},{12,8},{1,13},{5,1},{9,5},{13,9},{2,14},{6,2},{... | collective-permute-start | bytes 393224 | tf_op jit(solution)/shard_map/ppermute | solution.py:183
  146.0 2.3 %collective-permute-start.23 = (bf16[128,512]{1,0:T(8,128)(2,1)S(1)}, bf16[128,512]{1,0:T(8,128)(2,1)S(1)}, u32[]{:S(2)}, u32[]{:S(2)}) collective-permute-start(bf16[128,512]{1,0:T(8,128)(2,1)S(1)} %get-tuple-element.32), channel_id=1, source_target_pairs={{0,8},{4,12},{8,0},{12,4},{1,9},{5,13},{9,1},{13,5},{2,10},{6,14},... | collective-permute-start | bytes 393224 | tf_op jit(solution)/shard_map/ppermute | solution.py:183
  148.3 2.2 %collective-permute-done.17 = bf16[128,512]{1,0:T(8,128)(2,1)S(1)} collective-permute-done((bf16[128,512]{1,0:T(8,128)(2,1)S(1)}, bf16[128,512]{1,0:T(8,128)(2,1)S(1)}, u32[]{:S(2)}, u32[]{:S(2)}) %collective-permute-start.17) | collective-permute-done | bytes 131104 | tf_op jit(solution)/shard_map/ppermute | solution.py:183
  150.5 1.9 %fusion.5 = bf16[128,512]{1,0:T(8,128)(2,1)} fusion(bf16[128,512]{1,0:T(8,128)(2,1)S(1)} %collective-permute-done.18, bf16[128,512]{1,0:T(8,128)(2,1)S(1)} %collective-permute-done.17, bf16[128,512]{1,0:T(8,128)(2,1)S(1)} %collective-permute-done.16, bf16[4,128,512]{2,1,0:T(8,128)(2,1)} %collective-permute-done.15, ...), kind=kLoop, calls=%fused_computation.8 | loop fusion | flops 917504 | bytes 1048576 | tf_op jit(solution)/shard_map/convert_element_type | solution.py:211
  154.7 1.9 %fusion.2 = bf16[128,512]{1,0:T(8,128)(2,1)} fusion(bf16[128,512]{1,0:T(8,128)(2,1)S(1)} %collective-permute-done.24, bf16[128,512]{1,0:T(8,128)(2,1)S(1)} %collective-permute-done.23, bf16[128,512]{1,0:T(8,128)(2,1)S(1)} %collective-permute-done.22, bf16[4,128,512]{2,1,0:T(8,128)(2,1)} %collective-permute-done.21, ...), kind=kLoop, calls=%fused_computation.4 | loop fusion | flops 917504 | bytes 1048576 | tf_op jit(solution)/shard_map/convert_element_type | solution.py:211
  (83 shorter events, 20.2 us)
Async XLA Ops:
  7.2 68.9 %all-gather.3.cloned.1.call-start = ((), (), s32[]{:S(2)}) async-start(), calls=%async_computation.4 | async-start | bytes 4456448 | tf_op jit(solution)/shard_map/all_gather | solution.py:247
  16.3 114.8 %reduce-scatter.2.cloned.1.call-start = ((), (), s32[]{:S(2)}) async-start(), calls=%async_computation.3 | async-start | bytes 7077888 | tf_op jit(solution)/shard_map/reduce_scatter | solution.py:304
  43.4 12.4 %collective-permute-start.5 = (bf16[96,16,128]{2,1,0:T(8,128)(2,1)S(1)}, bf16[96,16,128]{2,1,0:T(8,128)(2,1)S(1)}, u32[]{:S(2)}, u32[]{:S(2)}) collective-permute-start(bf16[96,16,128]{2,1,0:T(8,128)(2,1)S(1)} %bitcast.81), channel_id=1, source_target_pairs={{0,96},{32,0},{64,32},{96,64},{1,97},{33,1},{65,33},{97,65},{2,98}... | collective-permute-start | bytes 1179656 | tf_op jit(solution)/shard_map/ppermute | solution.py:183
  46.3 13.3 %collective-permute-start.1 = (bf16[96,16,128]{2,1,0:T(8,128)(2,1)S(1)}, bf16[96,16,128]{2,1,0:T(8,128)(2,1)}, u32[]{:S(2)}, u32[]{:S(2)}) collective-permute-start(bf16[96,16,128]{2,1,0:T(8,128)(2,1)S(1)} %bitcast.82), channel_id=1, source_target_pairs={{0,32},{32,64},{64,96},{96,0},{1,33},{33,65},{65,97},{97,1},{2,34}... | collective-permute-start | bytes 1179656 | tf_op jit(solution)/shard_map/ppermute | solution.py:183
  46.3 14.7 %collective-permute-start.6 = (bf16[96,16,128]{2,1,0:T(8,128)(2,1)}, bf16[96,16,128]{2,1,0:T(8,128)(2,1)}, u32[]{:S(2)}, u32[]{:S(2)}) collective-permute-start(bf16[96,16,128]{2,1,0:T(8,128)(2,1)} %bitcast.17), channel_id=1, source_target_pairs={{0,96},{32,0},{64,32},{96,64},{1,97},{33,1},{65,33},{97,65},{2,98}... | collective-permute-start | bytes 1179656 | tf_op jit(solution)/shard_map/ppermute | solution.py:183
  49.5 19.5 %collective-permute-start.2 = (bf16[96,16,128]{2,1,0:T(8,128)(2,1)}, bf16[96,16,128]{2,1,0:T(8,128)(2,1)}, u32[]{:S(2)}, u32[]{:S(2)}) collective-permute-start(bf16[96,16,128]{2,1,0:T(8,128)(2,1)} %bitcast.17), channel_id=1, source_target_pairs={{0,32},{32,64},{64,96},{96,0},{1,33},{33,65},{65,97},{97,1},{2,34}... | collective-permute-start | bytes 1179656 | tf_op jit(solution)/shard_map/ppermute | solution.py:183
  55.8 14.4 %collective-permute-start.7 = (bf16[96,16,128]{2,1,0:T(8,128)(2,1)S(1)}, bf16[96,16,128]{2,1,0:T(8,128)(2,1)}, u32[]{:S(2)}, u32[]{:S(2)}) collective-permute-start(bf16[96,16,128]{2,1,0:T(8,128)(2,1)S(1)} %collective-permute-done.5.refs_6_), channel_id=1, source_target_pairs={{0,16},{16,0},{1,17},{17,1},{2,18},{18,2},{3,19},{19,3},{4,20},{20... | collective-permute-start | bytes 1179656 | tf_op jit(solution)/shard_map/ppermute | solution.py:183
  59.6 13.2 %collective-permute-start.9 = (bf16[96,16,128]{2,1,0:T(8,128)(2,1)}, bf16[96,16,128]{2,1,0:T(8,128)(2,1)}, u32[]{:S(2)}, u32[]{:S(2)}) collective-permute-start(bf16[96,16,128]{2,1,0:T(8,128)(2,1)} %collective-permute-done.1.refs_2_), channel_id=1, source_target_pairs={{0,32},{32,64},{64,96},{96,0},{1,33},{33,65},{65,97},{97,1},{2,34}... | collective-permute-start | bytes 1179656 | tf_op jit(solution)/shard_map/ppermute | solution.py:183
  59.6 13.3 %collective-permute-start.3 = (bf16[96,16,128]{2,1,0:T(8,128)(2,1)}, bf16[96,16,128]{2,1,0:T(8,128)(2,1)}, u32[]{:S(2)}, u32[]{:S(2)}) collective-permute-start(bf16[96,16,128]{2,1,0:T(8,128)(2,1)} %collective-permute-done.1.refs_2_), channel_id=1, source_target_pairs={{0,16},{16,0},{1,17},{17,1},{2,18},{18,2},{3,19},{19,3},{4,20},{20... | collective-permute-start | bytes 1179656 | tf_op jit(solution)/shard_map/ppermute | solution.py:183
  61.0 12.4 %collective-permute-start.10 = (bf16[96,16,128]{2,1,0:T(8,128)(2,1)}, bf16[96,16,128]{2,1,0:T(8,128)(2,1)}, u32[]{:S(2)}, u32[]{:S(2)}) collective-permute-start(bf16[96,16,128]{2,1,0:T(8,128)(2,1)} %collective-permute-done.6.refs_7_), channel_id=1, source_target_pairs={{0,96},{32,0},{64,32},{96,64},{1,97},{33,1},{65,33},{97,65},{2,98}... | collective-permute-start | bytes 1179656 | tf_op jit(solution)/shard_map/ppermute | solution.py:183
  69.0 7.1 %collective-permute-start = (bf16[192,16,128]{2,1,0:T(8,128)(2,1)S(1)}, bf16[192,16,128]{2,1,0:T(8,128)(2,1)}, u32[]{:S(2)}, u32[]{:S(2)}) collective-permute-start(bf16[192,16,128]{2,1,0:T(8,128)(2,1)S(1)} %bitcast.73), channel_id=1, source_target_pairs={{0,16},{16,0},{1,17},{17,1},{2,18},{18,2},{3,19},{19,3},{4,20},{20... | collective-permute-start | bytes 2359304 | tf_op jit(solution)/shard_map/ppermute | solution.py:183
  90.3 25.3 %collective-permute-start.13 = (bf16[4,128,512]{2,1,0:T(8,128)(2,1)}, bf16[4,128,512]{2,1,0:T(8,128)(2,1)S(1)}, u32[]{:S(2)}, u32[]{:S(2)}) collective-permute-start(bf16[4,128,512]{2,1,0:T(8,128)(2,1)} %get-tuple-element.19), channel_id=1, source_target_pairs={{0,12},{4,0},{8,4},{12,8},{1,13},{5,1},{9,5},{13,9},{2,14},{6,2},{... | collective-permute-start | bytes 1572872 | tf_op jit(solution)/shard_map/ppermute | solution.py:183
  92.2 23.4 %collective-permute-start.14 = (bf16[4,128,512]{2,1,0:T(8,128)(2,1)}, bf16[4,128,512]{2,1,0:T(8,128)(2,1)}, u32[]{:S(2)}, u32[]{:S(2)}) collective-permute-start(bf16[4,128,512]{2,1,0:T(8,128)(2,1)} %get-tuple-element.20), channel_id=1, source_target_pairs={{0,8},{4,12},{8,0},{12,4},{1,9},{5,13},{9,1},{13,5},{2,10},{6,14},... | collective-permute-start | bytes 1572872 | tf_op jit(solution)/shard_map/ppermute | solution.py:183
  92.2 26.7 %collective-permute-start.15 = (bf16[4,128,512]{2,1,0:T(8,128)(2,1)}, bf16[4,128,512]{2,1,0:T(8,128)(2,1)}, u32[]{:S(2)}, u32[]{:S(2)}) collective-permute-start(bf16[4,128,512]{2,1,0:T(8,128)(2,1)} %get-tuple-element.21), channel_id=1, source_target_pairs={{0,4},{4,8},{8,12},{12,0},{1,5},{5,9},{9,13},{13,1},{2,6},{6,10},{... | collective-permute-start | bytes 1572872 | tf_op jit(solution)/shard_map/ppermute | solution.py:183
  101.2 36.8 %collective-permute-start.19 = (bf16[4,128,512]{2,1,0:T(8,128)(2,1)}, bf16[4,128,512]{2,1,0:T(8,128)(2,1)}, u32[]{:S(2)}, u32[]{:S(2)}) collective-permute-start(bf16[4,128,512]{2,1,0:T(8,128)(2,1)} %get-tuple-element.24), channel_id=1, source_target_pairs={{0,3},{1,0},{2,1},{3,2},{4,7},{5,4},{6,5},{7,6},{8,11},{9,8},{10,9... | collective-permute-start | bytes 1572872 | tf_op jit(solution)/shard_map/ppermute | solution.py:183
  103.0 38.6 %collective-permute-start.20 = (bf16[4,128,512]{2,1,0:T(8,128)(2,1)}, bf16[4,128,512]{2,1,0:T(8,128)(2,1)}, u32[]{:S(2)}, u32[]{:S(2)}) collective-permute-start(bf16[4,128,512]{2,1,0:T(8,128)(2,1)} %get-tuple-element.25), channel_id=1, source_target_pairs={{0,2},{1,3},{2,0},{3,1},{4,6},{5,7},{6,4},{7,5},{8,10},{9,11},{10,... | collective-permute-start | bytes 1572872 | tf_op jit(solution)/shard_map/ppermute | solution.py:183
  115.6 26.0 %collective-permute-start.21 = (bf16[4,128,512]{2,1,0:T(8,128)(2,1)}, bf16[4,128,512]{2,1,0:T(8,128)(2,1)}, u32[]{:S(2)}, u32[]{:S(2)}) collective-permute-start(bf16[4,128,512]{2,1,0:T(8,128)(2,1)} %get-tuple-element.26), channel_id=1, source_target_pairs={{0,1},{1,2},{2,3},{3,0},{4,5},{5,6},{6,7},{7,4},{8,9},{9,10},{10,1... | collective-permute-start | bytes 1572872 | tf_op jit(solution)/shard_map/ppermute | solution.py:183
  121.1 24.9 %collective-permute-start.16 = (bf16[128,512]{1,0:T(8,128)(2,1)}, bf16[128,512]{1,0:T(8,128)(2,1)S(1)}, u32[]{:S(2)}, u32[]{:S(2)}) collective-permute-start(bf16[128,512]{1,0:T(8,128)(2,1)} %get-tuple-element.33), channel_id=1, source_target_pairs={{0,3},{1,0},{2,1},{3,2},{4,7},{5,4},{6,5},{7,6},{8,11},{9,8},{10,9... | collective-permute-start | bytes 393224 | tf_op jit(solution)/shard_map/ppermute | solution.py:183
  121.3 27.0 %collective-permute-start.18 = (bf16[128,512]{1,0:T(8,128)(2,1)}, bf16[128,512]{1,0:T(8,128)(2,1)S(1)}, u32[]{:S(2)}, u32[]{:S(2)}) collective-permute-start(bf16[128,512]{1,0:T(8,128)(2,1)} %get-tuple-element.34), channel_id=1, source_target_pairs={{0,1},{1,2},{2,3},{3,0},{4,5},{5,6},{6,7},{7,4},{8,9},{9,10},{10,1... | collective-permute-start | bytes 393224 | tf_op jit(solution)/shard_map/ppermute | solution.py:183
  131.2 25.4 %all-to-all-start.1 = ((bf16[16,3,4,16,128]{4,3,2,1,0:T(8,128)(2,1)}), bf16[16,3,4,16,128]{4,3,2,1,0:T(8,128)(2,1)S(1)}, u32[]{:S(2)}, u32[]{:S(2)}) async-start(bf16[16,3,4,16,128]{4,3,2,1,0:T(8,128)(2,1)} %bitcast.80), calls=%async_computation.2 | async-start | bytes 1572864 | tf_op jit(solution)/shard_map/all_to_all | solution.py:325
  138.1 12.4 %collective-permute-start.17 = (bf16[128,512]{1,0:T(8,128)(2,1)S(1)}, bf16[128,512]{1,0:T(8,128)(2,1)S(1)}, u32[]{:S(2)}, u32[]{:S(2)}) collective-permute-start(bf16[128,512]{1,0:T(8,128)(2,1)S(1)} %get-tuple-element.35), channel_id=1, source_target_pairs={{0,2},{1,3},{2,0},{3,1},{4,6},{5,7},{6,4},{7,5},{8,10},{9,11},{10,... | collective-permute-start | bytes 393224 | tf_op jit(solution)/shard_map/ppermute | solution.py:183
  143.2 9.1 %collective-permute-start.22 = (bf16[128,512]{1,0:T(8,128)(2,1)S(1)}, bf16[128,512]{1,0:T(8,128)(2,1)S(1)}, u32[]{:S(2)}, u32[]{:S(2)}) collective-permute-start(bf16[128,512]{1,0:T(8,128)(2,1)S(1)} %get-tuple-element.30), channel_id=1, source_target_pairs={{0,12},{4,0},{8,4},{12,8},{1,13},{5,1},{9,5},{13,9},{2,14},{6,2},{... | collective-permute-start | bytes 393224 | tf_op jit(solution)/shard_map/ppermute | solution.py:183
  146.0 7.3 %collective-permute-start.24 = (bf16[128,512]{1,0:T(8,128)(2,1)S(1)}, bf16[128,512]{1,0:T(8,128)(2,1)S(1)}, u32[]{:S(2)}, u32[]{:S(2)}) collective-permute-start(bf16[128,512]{1,0:T(8,128)(2,1)S(1)} %get-tuple-element.31), channel_id=1, source_target_pairs={{0,4},{4,8},{8,12},{12,0},{1,5},{5,9},{9,13},{13,1},{2,6},{6,10},{... | collective-permute-start | bytes 393224 | tf_op jit(solution)/shard_map/ppermute | solution.py:183
  146.0 8.7 %collective-permute-start.23 = (bf16[128,512]{1,0:T(8,128)(2,1)S(1)}, bf16[128,512]{1,0:T(8,128)(2,1)S(1)}, u32[]{:S(2)}, u32[]{:S(2)}) collective-permute-start(bf16[128,512]{1,0:T(8,128)(2,1)S(1)} %get-tuple-element.32), channel_id=1, source_target_pairs={{0,8},{4,12},{8,0},{12,4},{1,9},{5,13},{9,1},{13,5},{2,10},{6,14},... | collective-permute-start | bytes 393224 | tf_op jit(solution)/shard_map/ppermute | solution.py:183
  (12 other events, 221.7 us)
Sparse Core Ops, SparseCore 0:
  16.4 56.5 all-gather.2
  90.5 40.6 reduce-scatter.1
where the time goes:
time: 165 us; the launch traced here: 164 us
  waiting for transfers between devices  41.3 us (25%)
  starting transfers between devices  34.2 us (21%)
  Pallas kernels  31.1 us (19%)
  blocking collectives  24.7 us (15%)
  between operations  14.3 us (9%)
  other arithmetic  9.86 us (6%)
  local copies, waits for them, and re-layouts  8.89 us (5%)
    ppermute x25, waiting for transfers between devices, shift(): lax.ppermute(value, axis, [(i, (i + hop) % size) for i in range(size)])  33.2 us
    ppermute x25, starting transfers between devices, shift(): lax.ppermute(value, axis, [(i, (i + hop) % size) for i in range(size)])  27.2 us
    all_to_all x1, blocking collectives, body(): mine = lax.all_to_all(slabs, MP, split_axis=0, concat_axis=0, tiled=True)  24.7 us
    pallas_call x1, Pallas kernels, body(): pl.pallas_call(functools.partial(owner_kernel, owned=owned, **sizes), out...  14.2 us
    pallas_call x1, Pallas kernels, body(): pl.pallas_call(pair_kernel, out_shape=jax.ShapeDtypeStruct((2,) + tokens....  9.06 us
    reduce_scatter x1, waiting for transfers between devices, body(): grads = lax.psum_scatter(grads, DP, scatter_dimension=0, tiled=True)  8.03 us
    pallas_call x1, Pallas kernels, parts_of(): pl.pallas_call(functools.partial(parts_kernel, projections=projections, *...  7.87 us
    all_to_all x1, starting transfers between devices, body(): grads = lax.all_to_all(grads, MP, split_axis=0, concat_axis=0, tiled=True)  6.89 us
  transfers between devices with their start and end apart: 28, of which 10 were waited for; matrix products, arithmetic and copies ran while one was open for 11% of the time, Pallas kernels for 5%

commit v1 on v0

--- a/solution.py
+++ b/solution.py
@@ -174,10 +174,6 @@
     wait_all(send_parts(acc, stage, outs, sems, count, per, projections[0] == 2))
 
 
-def pair_kernel(a, b, out, sems):
-    wait_all(start_all([(a, out.at[0]), (b, out.at[1])], sems, 0))
-
-
 def shift(value, axis, hop):
     size = lax.axis_size(axis)
     return lax.ppermute(value, axis, [(i, (i + hop) % size) for i in range(size)])
@@ -201,15 +197,17 @@
     return pieces
 
 
-def collect(outs, grads):
+def collect(outs, grads, other):
     ring = len(outs)
     first = [[p[0]] + [shift(p[h], a, -h) for h in range(1, ring)] for p, a in ((outs, "x"), (grads, "z"))]
+    sums = [[total(*[t[turn] for t in terms]) for turn in range(ring)] for terms in first]
+    moved = [[v.astype(BF) for v in s[1:]] for s in sums]
+    moved[1], other = lax.optimization_barrier((moved[1], other))
     done = []
-    for terms, axis in zip(first, ("z", "x")):
-        sums = [total(*[t[turn] for t in terms]) for turn in range(ring)]
-        arrived = [shift(sums[turn].astype(BF), axis, -turn) for turn in range(1, ring)]
-        done.append(total(sums[0], *arrived).astype(BF))
-    return done
+    for s, m, axis in zip(sums, moved, ("z", "x")):
+        arrived = [shift(m[turn - 1], axis, -turn) for turn in range(1, ring)]
+        done.append(total(s[0], *arrived).astype(BF))
+    return done, other
 
 
 def body(
@@ -236,15 +234,7 @@
     count = 3 * held
     tok = tokens.shape[0]
 
-    pair = pl.pallas_call(
-        pair_kernel,
-        out_shape=jax.ShapeDtypeStruct((2,) + tokens.shape, BF),
-        in_specs=[ANY] * 2,
-        out_specs=ANY,
-        scratch_shapes=[pltpu.SemaphoreType.DMA((2,))],
-        name="pair",
-    )(tokens, grad_out)
-    x_all = lax.all_gather(pair, MP, axis=0, tiled=False)
+    x_all = lax.all_gather(jnp.stack([tokens, grad_out]), MP, axis=0, tiled=False)
 
     slabs = jnp.stack(
         [
@@ -320,7 +310,7 @@
         )(hops, cols, slots, act, *by_share)
 
     in_parts = parts_of((0, 1))
-    output, input_grad = collect(out_parts, in_parts)
+    (output, input_grad), grads = collect(out_parts, in_parts, grads)
     grads = grads.reshape(n_mp, 3, quota, slab, BS)
     grads = lax.all_to_all(grads, MP, split_axis=0, concat_axis=0, tiled=True)
     gate_grad, up_grad, down_grad = (grads[:, p].reshape(held, slab, BS) for p in range(3))

time: 165 us -> 162 us (0.982)
  Pallas kernels: 31.1 us -> 22 us
  waiting for transfers between devices: 41.3 us -> 47.6 us
    ppermute x25, waiting for transfers between devices: 33.2 us -> 45 us  [shift(): lax.ppermute(value, axis, [(i, (i + hop) % size) for i in range(size)])]
    pallas_call x1 -> x0, Pallas kernels: 9.06 us -> none  [body(): pl.pallas_call(pair_kernel, out_shape=jax.ShapeDtypeStruct((2,) + tokens....]
    reduce_scatter x1, waiting for transfers between devices: 8.03 us -> 2.58 us  [body(): grads = lax.psum_scatter(grads, DP, scatter_dimension=0, tiled=True)]
    another operation x0 -> x1, other arithmetic: none -> 1.84 us  [body(): jnp.stack([tokens, grad_out])]
where the time goes in v1:
time: 162 us
  waiting for transfers between devices  47.6 us (29%)
  starting transfers between devices  32.8 us (20%)
  blocking collectives  23.7 us (15%)
  Pallas kernels  22 us (14%)
  between operations  14.3 us (9%)
  other arithmetic  11.5 us (7%)
  local copies, waits for them, and re-layouts  9.76 us (6%)
    ppermute x25, waiting for transfers between devices, shift(): lax.ppermute(value, axis, [(i, (i + hop) % size) for i in range(size)])  45 us
    ppermute x25, starting transfers between devices, shift(): lax.ppermute(value, axis, [(i, (i + hop) % size) for i in range(size)])  26.1 us
    all_to_all x1, blocking collectives, body(): mine = lax.all_to_all(slabs, MP, split_axis=0, concat_axis=0, tiled=True)  23.7 us
    pallas_call x1, Pallas kernels, body(): pl.pallas_call(functools.partial(owner_kernel, owned=owned, **sizes), out...  14.2 us
    pallas_call x1, Pallas kernels, parts_of(): pl.pallas_call(functools.partial(parts_kernel, projections=projections, *...  7.84 us
    all_to_all x1, starting transfers between devices, body(): grads = lax.all_to_all(grads, MP, split_axis=0, concat_axis=0, tiled=True)  6.62 us
    another operation x6, local copies, waits for them, and re-layouts, body(): tables = jnp.stack([gate_block_pairs, up_blocks, down_blocks])  4.24 us
    convert_element_type x2, other arithmetic, collect(): done.append(total(s[0], *arrived).astype(BF))  3.74 us
  transfers between devices with their start and end apart: 28, of which 10 were waited for; matrix products, arithmetic and copies ran while one was open for 11% of the time, Pallas kernels for 5%

profile of v1, /device:TPU:0, one launch (start us, length us, event | category | flops | bytes accessed | tf_op | source)
XLA Modules:
  0.0 161.6 jit_solution(17835964719764190842)
XLA Ops:
  7.2 1.8 %pad_maximum_fusion.1 = bf16[2,128,512]{2,1,0:T(8,128)(2,1)} fusion(bf16[1,128,512]{2,1,0:T(8,128)(2,1)} %bitcast.88, bf16[1,128,512]{2,1,0:T(8,128)(2,1)} %bitcast.89), kind=kLoop, calls=%fused_computation.1 | loop fusion | flops 131072 | bytes 524288 | tf_op jit(solution)/shard_map/stack | solution.py:237
  10.4 23.7 %all_to_all.10.refs_0_ = bf16[16,3,4,16,128]{4,3,2,1,0:T(8,128)(2,1)S(1)} all-to-all(bf16[16,3,4,16,128]{4,3,2,1,0:T(8,128)(2,1)S(1)} %pad_maximum_fusion), channel_id=1, replica_groups=mesh['y'=4,'c'=2,'x'=4,'z'=4] {'x','z'}, dimensions={0} | all-to-all | bytes 1572864 | tf_op jit(solution)/shard_map/all_to_all | solution.py:246
  35.1 3.1 %collective-permute-start.5 = (bf16[96,16,128]{2,1,0:T(8,128)(2,1)S(1)}, bf16[96,16,128]{2,1,0:T(8,128)(2,1)S(1)}, u32[]{:S(2)}, u32[]{:S(2)}) collective-permute-start(bf16[96,16,128]{2,1,0:T(8,128)(2,1)S(1)} %bitcast.83), channel_id=1, source_target_pairs={{0,96},{32,0},{64,32},{96,64},{1,97},{33,1},{65,33},{97,65},{2,98}... | collective-permute-start | bytes 1179656 | tf_op jit(solution)/shard_map/ppermute | solution.py:179
  38.2 3.2 %collective-permute-start.6 = (bf16[96,16,128]{2,1,0:T(8,128)(2,1)}, bf16[96,16,128]{2,1,0:T(8,128)(2,1)}, u32[]{:S(2)}, u32[]{:S(2)}) collective-permute-start(bf16[96,16,128]{2,1,0:T(8,128)(2,1)} %bitcast.19), channel_id=1, source_target_pairs={{0,96},{32,0},{64,32},{96,64},{1,97},{33,1},{65,33},{97,65},{2,98}... | collective-permute-start | bytes 1179656 | tf_op jit(solution)/shard_map/ppermute | solution.py:179
  41.4 6.3 %collective-permute-done.5.refs_6_ = bf16[96,16,128]{2,1,0:T(8,128)(2,1)S(1)} collective-permute-done((bf16[96,16,128]{2,1,0:T(8,128)(2,1)S(1)}, bf16[96,16,128]{2,1,0:T(8,128)(2,1)S(1)}, u32[]{:S(2)}, u32[]{:S(2)}) %collective-permute-start.5) | collective-permute-done | bytes 393248 | tf_op jit(solution)/shard_map/ppermute | solution.py:179
  47.7 3.8 %collective-permute-done.1.refs_2_ = bf16[96,16,128]{2,1,0:T(8,128)(2,1)} collective-permute-done((bf16[96,16,128]{2,1,0:T(8,128)(2,1)S(1)}, bf16[96,16,128]{2,1,0:T(8,128)(2,1)}, u32[]{:S(2)}, u32[]{:S(2)}) %collective-permute-start.1) | collective-permute-done | bytes 393248 | tf_op jit(solution)/shard_map/ppermute | solution.py:179
  52.5 3.7 %collective-permute-start.10 = (bf16[96,16,128]{2,1,0:T(8,128)(2,1)}, bf16[96,16,128]{2,1,0:T(8,128)(2,1)}, u32[]{:S(2)}, u32[]{:S(2)}) collective-permute-start(bf16[96,16,128]{2,1,0:T(8,128)(2,1)} %collective-permute-done.6.refs_7_), channel_id=1, source_target_pairs={{0,96},{32,0},{64,32},{96,64},{1,97},{33,1},{65,33},{97,65},{2,98}... | collective-permute-start | bytes 1179656 | tf_op jit(solution)/shard_map/ppermute | solution.py:179
  62.3 2.0 %collective-permute-done.9.refs_10_ = bf16[96,16,128]{2,1,0:T(8,128)(2,1)} collective-permute-done((bf16[96,16,128]{2,1,0:T(8,128)(2,1)}, bf16[96,16,128]{2,1,0:T(8,128)(2,1)}, u32[]{:S(2)}, u32[]{:S(2)}) %collective-permute-start.9) | collective-permute-done | bytes 393248 | tf_op jit(solution)/shard_map/ppermute | solution.py:179
  67.9 14.2 %owner.1 = (bf16[3,7,128,128]{3,2,1,0:T(8,128)(2,1)}, bf16[128,896]{1,0:T(8,128)(2,1)}, bf16[8,192,16,128]{3,2,1,0:T(8,128)(2,1)}, bf16[4,128,512]{2,1,0:T(8,128...) custom-call(s32[192]{0:T(256)} %get-tuple-element.37.rows, ...), custom_call_target="tpu_custom_call" | custom-call | tf_op jit(solution)/shard_map/owner/pallas_call | solution.py:273
  82.1 7.8 %shard_map.136 = (bf16[4,128,512]{2,1,0:T(8,128)(2,1)}, bf16[4,128,512]{2,1,0:T(8,128)(2,1)}, bf16[4,128,512]{2,1,0:T(8,128)(2,1)}, bf16[4,128,512]{2,1,0:T(8,128)(2,1)}) custom-call(s32[192]{0:T(256)} %get-tuple-element.36.hops.rows, s32[192]{0:T(256)} %select_reduce_fusion.cols, s32[8]{0:T(128)} %stack.63.slots, ...), custom_call_target="tpu_custom_call" | custom-call | tf_op jit(solution)/shard_map/pallas_call | solution.py:299
  89.9 2.0 %collective-permute-start.19 = (bf16[4,128,512]{2,1,0:T(8,128)(2,1)}, bf16[4,128,512]{2,1,0:T(8,128)(2,1)S(1)}, u32[]{:S(2)}, u32[]{:S(2)}) collective-permute-start(bf16[4,128,512]{2,1,0:T(8,128)(2,1)} %get-tuple-element.28), channel_id=1, source_target_pairs={{0,3},{1,0},{2,1},{3,2},{4,7},{5,4},{6,5},{7,6},{8,11},{9,8},{10,9... | collective-permute-start | bytes 1572872 | tf_op jit(solution)/shard_map/ppermute | solution.py:179
  95.5 19.6 %collective-permute-done.19 = bf16[4,128,512]{2,1,0:T(8,128)(2,1)S(1)} collective-permute-done((bf16[4,128,512]{2,1,0:T(8,128)(2,1)}, bf16[4,128,512]{2,1,0:T(8,128)(2,1)S(1)}, u32[]{:S(2)}, u32[]{:S(2)}) %collective-permute-start.19) | collective-permute-done | bytes 524320 | tf_op jit(solution)/shard_map/ppermute | solution.py:179
  115.1 3.6 %collective-permute-done.21 = bf16[4,128,512]{2,1,0:T(8,128)(2,1)S(1)} collective-permute-done((bf16[4,128,512]{2,1,0:T(8,128)(2,1)}, bf16[4,128,512]{2,1,0:T(8,128)(2,1)S(1)}, u32[]{:S(2)}, u32[]{:S(2)}) %collective-permute-start.21) | collective-permute-done | bytes 524320 | tf_op jit(solution)/shard_map/ppermute | solution.py:179
  119.5 1.9 %fusion.11 = (bf16[128,512]{1,0:T(8,128)(2,1)S(1)}, bf16[128,512]{1,0:T(8,128)(2,1)S(1)}, bf16[128,512]{1,0:T(8,128)(2,1)}) fusion(bf16[4,128,512]{2,1,0:T(8,128)(2,1)S(1)} %collective-permute-done.21, bf16[4,128,512]{2,1,0:T(8,128)(2,1)S(1)} %collective-permute-done.20, bf16[4,128,512]{2,1,0:T(8,128)(2,1)S(1)} %collective-permute-done.19, ...), kind=kLoop, calls=%fused_computation.23 | loop fusion | flops 1572864 | bytes 1966080 | tf_op jit(solution)/shard_map/add | solution.py:183
  121.4 2.6 %reduce-scatter.2.cloned.1.call-done = bf16[1,192,16,128]{3,2,1,0:T(8,128)(2,1)} async-done(((bf16[8,192,16,128]{3,2,1,0:T(8,128)(2,1)}), bf16[1,192,16,128]{3,2,1,0:T(8,128)(2,1)}) %reduce-scatter.2.cloned.1.call-update) | async-done | bytes 786448 | tf_op jit(solution)/shard_map/reduce_scatter | solution.py:294
  124.0 6.6 %all-to-all-start.1 = ((bf16[16,3,4,16,128]{4,3,2,1,0:T(8,128)(2,1)}), bf16[16,3,4,16,128]{4,3,2,1,0:T(8,128)(2,1)S(1)}, u32[]{:S(2)}, u32[]{:S(2)}) async-start(bf16[16,3,4,16,128]{4,3,2,1,0:T(8,128)(2,1)} %bitcast.82), calls=%async_computation.2 | async-start | bytes 1572864 | tf_op jit(solution)/shard_map/all_to_all | solution.py:315
  132.3 3.2 %collective-permute-start.16 = (bf16[128,512]{1,0:T(8,128)(2,1)S(1)}, bf16[128,512]{1,0:T(8,128)(2,1)S(1)}, u32[]{:S(2)}, u32[]{:S(2)}) collective-permute-start(bf16[128,512]{1,0:T(8,128)(2,1)S(1)} %get-tuple-element.41), channel_id=1, source_target_pairs={{0,3},{1,0},{2,1},{3,2},{4,7},{5,4},{6,5},{7,6},{8,11},{9,8},{10,9... | collective-permute-start | bytes 393224 | tf_op jit(solution)/shard_map/ppermute | solution.py:179
  135.5 2.3 %collective-permute-start.17 = (bf16[128,512]{1,0:T(8,128)(2,1)S(1)}, bf16[128,512]{1,0:T(8,128)(2,1)S(1)}, u32[]{:S(2)}, u32[]{:S(2)}) collective-permute-start(bf16[128,512]{1,0:T(8,128)(2,1)S(1)} %get-tuple-element.43), channel_id=1, source_target_pairs={{0,2},{1,3},{2,0},{3,1},{4,6},{5,7},{6,4},{7,5},{8,10},{9,11},{10,... | collective-permute-start | bytes 393224 | tf_op jit(solution)/shard_map/ppermute | solution.py:179
  137.8 2.7 %collective-permute-start.22 = (bf16[128,512]{1,0:T(8,128)(2,1)}, bf16[128,512]{1,0:T(8,128)(2,1)S(1)}, u32[]{:S(2)}, u32[]{:S(2)}) collective-permute-start(bf16[128,512]{1,0:T(8,128)(2,1)} %get-tuple-element.32), channel_id=1, source_target_pairs={{0,12},{4,0},{8,4},{12,8},{1,13},{5,1},{9,5},{13,9},{2,14},{6,2},{... | collective-permute-start | bytes 393224 | tf_op jit(solution)/shard_map/ppermute | solution.py:179
  141.4 4.5 %collective-permute-done.16 = bf16[128,512]{1,0:T(8,128)(2,1)S(1)} collective-permute-done((bf16[128,512]{1,0:T(8,128)(2,1)S(1)}, bf16[128,512]{1,0:T(8,128)(2,1)S(1)}, u32[]{:S(2)}, u32[]{:S(2)}) %collective-permute-start.16) | collective-permute-done | bytes 131104 | tf_op jit(solution)/shard_map/ppermute | solution.py:179
  145.9 2.5 %collective-permute-done.17 = bf16[128,512]{1,0:T(8,128)(2,1)S(1)} collective-permute-done((bf16[128,512]{1,0:T(8,128)(2,1)S(1)}, bf16[128,512]{1,0:T(8,128)(2,1)S(1)}, u32[]{:S(2)}, u32[]{:S(2)}) %collective-permute-start.17) | collective-permute-done | bytes 131104 | tf_op jit(solution)/shard_map/ppermute | solution.py:179
  148.4 1.9 %fusion.5 = bf16[128,512]{1,0:T(8,128)(2,1)} fusion(bf16[128,512]{1,0:T(8,128)(2,1)S(1)} %collective-permute-done.18, bf16[128,512]{1,0:T(8,128)(2,1)S(1)} %collective-permute-done.17, bf16[128,512]{1,0:T(8,128)(2,1)S(1)} %collective-permute-done.16, bf16[4,128,512]{2,1,0:T(8,128)(2,1)} %collective-permute-done.15, ...), kind=kLoop, calls=%fused_computation.9 | loop fusion | flops 917504 | bytes 1048576 | tf_op jit(solution)/shard_map/convert_element_type | solution.py:209
  150.3 1.7 %collective-permute-done.24 = bf16[128,512]{1,0:T(8,128)(2,1)S(1)} collective-permute-done((bf16[128,512]{1,0:T(8,128)(2,1)S(1)}, bf16[128,512]{1,0:T(8,128)(2,1)S(1)}, u32[]{:S(2)}, u32[]{:S(2)}) %collective-permute-start.24) | collective-permute-done | bytes 131104 | tf_op jit(solution)/shard_map/ppermute | solution.py:179
  152.0 1.9 %fusion.2 = bf16[128,512]{1,0:T(8,128)(2,1)} fusion(bf16[128,512]{1,0:T(8,128)(2,1)S(1)} %collective-permute-done.24, bf16[128,512]{1,0:T(8,128)(2,1)S(1)} %collective-permute-done.23, bf16[128,512]{1,0:T(8,128)(2,1)S(1)} %collective-permute-done.22, bf16[4,128,512]{2,1,0:T(8,128)(2,1)} %copy-done.5, bf16[4,128,512]{2,1,0:T(8,128)(2,1)} %copy-done.4, ...), kind=kLoop, calls=%fused_computation.5 | loop fusion | flops 917504 | bytes 1048576 | tf_op jit(solution)/shard_map/convert_element_type | solution.py:209
  (85 shorter events, 20.8 us)
Async XLA Ops:
  7.2 60.7 %all-gather.3.cloned.1.call-start = ((), (), s32[]{:S(2)}) async-start(), calls=%async_computation.4 | async-start | bytes 4456448 | tf_op jit(solution)/shard_map/all_gather | solution.py:237
  9.1 114.9 %reduce-scatter.2.cloned.1.call-start = ((), (), s32[]{:S(2)}) async-start(), calls=%async_computation.3 | async-start | bytes 7077888 | tf_op jit(solution)/shard_map/reduce_scatter | solution.py:294
  35.1 12.6 %collective-permute-start.5 = (bf16[96,16,128]{2,1,0:T(8,128)(2,1)S(1)}, bf16[96,16,128]{2,1,0:T(8,128)(2,1)S(1)}, u32[]{:S(2)}, u32[]{:S(2)}) collective-permute-start(bf16[96,16,128]{2,1,0:T(8,128)(2,1)S(1)} %bitcast.83), channel_id=1, source_target_pairs={{0,96},{32,0},{64,32},{96,64},{1,97},{33,1},{65,33},{97,65},{2,98}... | collective-permute-start | bytes 1179656 | tf_op jit(solution)/shard_map/ppermute | solution.py:179
  38.2 13.3 %collective-permute-start.1 = (bf16[96,16,128]{2,1,0:T(8,128)(2,1)S(1)}, bf16[96,16,128]{2,1,0:T(8,128)(2,1)}, u32[]{:S(2)}, u32[]{:S(2)}) collective-permute-start(bf16[96,16,128]{2,1,0:T(8,128)(2,1)S(1)} %bitcast.84), channel_id=1, source_target_pairs={{0,32},{32,64},{64,96},{96,0},{1,33},{33,65},{65,97},{97,1},{2,34}... | collective-permute-start | bytes 1179656 | tf_op jit(solution)/shard_map/ppermute | solution.py:179
  38.2 14.3 %collective-permute-start.6 = (bf16[96,16,128]{2,1,0:T(8,128)(2,1)}, bf16[96,16,128]{2,1,0:T(8,128)(2,1)}, u32[]{:S(2)}, u32[]{:S(2)}) collective-permute-start(bf16[96,16,128]{2,1,0:T(8,128)(2,1)} %bitcast.19), channel_id=1, source_target_pairs={{0,96},{32,0},{64,32},{96,64},{1,97},{33,1},{65,33},{97,65},{2,98}... | collective-permute-start | bytes 1179656 | tf_op jit(solution)/shard_map/ppermute | solution.py:179
  41.4 19.1 %collective-permute-start.2 = (bf16[96,16,128]{2,1,0:T(8,128)(2,1)}, bf16[96,16,128]{2,1,0:T(8,128)(2,1)}, u32[]{:S(2)}, u32[]{:S(2)}) collective-permute-start(bf16[96,16,128]{2,1,0:T(8,128)(2,1)} %bitcast.19), channel_id=1, source_target_pairs={{0,32},{32,64},{64,96},{96,0},{1,33},{33,65},{65,97},{97,1},{2,34}... | collective-permute-start | bytes 1179656 | tf_op jit(solution)/shard_map/ppermute | solution.py:179
  47.7 14.0 %collective-permute-start.7 = (bf16[96,16,128]{2,1,0:T(8,128)(2,1)S(1)}, bf16[96,16,128]{2,1,0:T(8,128)(2,1)}, u32[]{:S(2)}, u32[]{:S(2)}) collective-permute-start(bf16[96,16,128]{2,1,0:T(8,128)(2,1)S(1)} %collective-permute-done.5.refs_6_), channel_id=1, source_target_pairs={{0,16},{16,0},{1,17},{17,1},{2,18},{18,2},{3,19},{19,3},{4,20},{20... | collective-permute-start | bytes 1179656 | tf_op jit(solution)/shard_map/ppermute | solution.py:179
  51.5 12.8 %collective-permute-start.9 = (bf16[96,16,128]{2,1,0:T(8,128)(2,1)}, bf16[96,16,128]{2,1,0:T(8,128)(2,1)}, u32[]{:S(2)}, u32[]{:S(2)}) collective-permute-start(bf16[96,16,128]{2,1,0:T(8,128)(2,1)} %collective-permute-done.1.refs_2_), channel_id=1, source_target_pairs={{0,32},{32,64},{64,96},{96,0},{1,33},{33,65},{65,97},{97,1},{2,34}... | collective-permute-start | bytes 1179656 | tf_op jit(solution)/shard_map/ppermute | solution.py:179
  51.5 12.9 %collective-permute-start.3 = (bf16[96,16,128]{2,1,0:T(8,128)(2,1)}, bf16[96,16,128]{2,1,0:T(8,128)(2,1)}, u32[]{:S(2)}, u32[]{:S(2)}) collective-permute-start(bf16[96,16,128]{2,1,0:T(8,128)(2,1)} %collective-permute-done.1.refs_2_), channel_id=1, source_target_pairs={{0,16},{16,0},{1,17},{17,1},{2,18},{18,2},{3,19},{19,3},{4,20},{20... | collective-permute-start | bytes 1179656 | tf_op jit(solution)/shard_map/ppermute | solution.py:179
  52.5 12.4 %collective-permute-start.10 = (bf16[96,16,128]{2,1,0:T(8,128)(2,1)}, bf16[96,16,128]{2,1,0:T(8,128)(2,1)}, u32[]{:S(2)}, u32[]{:S(2)}) collective-permute-start(bf16[96,16,128]{2,1,0:T(8,128)(2,1)} %collective-permute-done.6.refs_7_), channel_id=1, source_target_pairs={{0,96},{32,0},{64,32},{96,64},{1,97},{33,1},{65,33},{97,65},{2,98}... | collective-permute-start | bytes 1179656 | tf_op jit(solution)/shard_map/ppermute | solution.py:179
  60.5 7.3 %collective-permute-start = (bf16[192,16,128]{2,1,0:T(8,128)(2,1)S(1)}, bf16[192,16,128]{2,1,0:T(8,128)(2,1)}, u32[]{:S(2)}, u32[]{:S(2)}) collective-permute-start(bf16[192,16,128]{2,1,0:T(8,128)(2,1)S(1)} %bitcast.75), channel_id=1, source_target_pairs={{0,16},{16,0},{1,17},{17,1},{2,18},{18,2},{3,19},{19,3},{4,20},{20... | collective-permute-start | bytes 2359304 | tf_op jit(solution)/shard_map/ppermute | solution.py:179
  89.9 25.2 %collective-permute-start.19 = (bf16[4,128,512]{2,1,0:T(8,128)(2,1)}, bf16[4,128,512]{2,1,0:T(8,128)(2,1)S(1)}, u32[]{:S(2)}, u32[]{:S(2)}) collective-permute-start(bf16[4,128,512]{2,1,0:T(8,128)(2,1)} %get-tuple-element.28), channel_id=1, source_target_pairs={{0,3},{1,0},{2,1},{3,2},{4,7},{5,4},{6,5},{7,6},{8,11},{9,8},{10,9... | collective-permute-start | bytes 1572872 | tf_op jit(solution)/shard_map/ppermute | solution.py:179
  91.9 23.2 %collective-permute-start.20 = (bf16[4,128,512]{2,1,0:T(8,128)(2,1)}, bf16[4,128,512]{2,1,0:T(8,128)(2,1)S(1)}, u32[]{:S(2)}, u32[]{:S(2)}) collective-permute-start(bf16[4,128,512]{2,1,0:T(8,128)(2,1)} %get-tuple-element.29), channel_id=1, source_target_pairs={{0,2},{1,3},{2,0},{3,1},{4,6},{5,7},{6,4},{7,5},{8,10},{9,11},{10,... | collective-permute-start | bytes 1572872 | tf_op jit(solution)/shard_map/ppermute | solution.py:179
  92.5 26.2 %collective-permute-start.21 = (bf16[4,128,512]{2,1,0:T(8,128)(2,1)}, bf16[4,128,512]{2,1,0:T(8,128)(2,1)S(1)}, u32[]{:S(2)}, u32[]{:S(2)}) collective-permute-start(bf16[4,128,512]{2,1,0:T(8,128)(2,1)} %get-tuple-element.30), channel_id=1, source_target_pairs={{0,1},{1,2},{2,3},{3,0},{4,5},{5,6},{6,7},{7,4},{8,9},{9,10},{10,1... | collective-permute-start | bytes 1572872 | tf_op jit(solution)/shard_map/ppermute | solution.py:179
  93.7 36.9 %collective-permute-start.13 = (bf16[4,128,512]{2,1,0:T(8,128)(2,1)}, bf16[4,128,512]{2,1,0:T(8,128)(2,1)}, u32[]{:S(2)}, u32[]{:S(2)}) collective-permute-start(bf16[4,128,512]{2,1,0:T(8,128)(2,1)} %get-tuple-element.23), channel_id=1, source_target_pairs={{0,12},{4,0},{8,4},{12,8},{1,13},{5,1},{9,5},{13,9},{2,14},{6,2},{... | collective-permute-start | bytes 1572872 | tf_op jit(solution)/shard_map/ppermute | solution.py:179
  94.8 35.9 %collective-permute-start.14 = (bf16[4,128,512]{2,1,0:T(8,128)(2,1)}, bf16[4,128,512]{2,1,0:T(8,128)(2,1)}, u32[]{:S(2)}, u32[]{:S(2)}) collective-permute-start(bf16[4,128,512]{2,1,0:T(8,128)(2,1)} %get-tuple-element.24), channel_id=1, source_target_pairs={{0,8},{4,12},{8,0},{12,4},{1,9},{5,13},{9,1},{13,5},{2,10},{6,14},... | collective-permute-start | bytes 1572872 | tf_op jit(solution)/shard_map/ppermute | solution.py:179
  115.1 15.6 %collective-permute-start.15 = (bf16[4,128,512]{2,1,0:T(8,128)(2,1)}, bf16[4,128,512]{2,1,0:T(8,128)(2,1)}, u32[]{:S(2)}, u32[]{:S(2)}) collective-permute-start(bf16[4,128,512]{2,1,0:T(8,128)(2,1)} %get-tuple-element.25), channel_id=1, source_target_pairs={{0,4},{4,8},{8,12},{12,0},{1,5},{5,9},{9,13},{13,1},{2,6},{6,10},{... | collective-permute-start | bytes 1572872 | tf_op jit(solution)/shard_map/ppermute | solution.py:179
  124.0 29.9 %all-to-all-start.1 = ((bf16[16,3,4,16,128]{4,3,2,1,0:T(8,128)(2,1)}), bf16[16,3,4,16,128]{4,3,2,1,0:T(8,128)(2,1)S(1)}, u32[]{:S(2)}, u32[]{:S(2)}) async-start(bf16[16,3,4,16,128]{4,3,2,1,0:T(8,128)(2,1)} %bitcast.82), calls=%async_computation.2 | async-start | bytes 1572864 | tf_op jit(solution)/shard_map/all_to_all | solution.py:315
  132.3 13.5 %collective-permute-start.16 = (bf16[128,512]{1,0:T(8,128)(2,1)S(1)}, bf16[128,512]{1,0:T(8,128)(2,1)S(1)}, u32[]{:S(2)}, u32[]{:S(2)}) collective-permute-start(bf16[128,512]{1,0:T(8,128)(2,1)S(1)} %get-tuple-element.41), channel_id=1, source_target_pairs={{0,3},{1,0},{2,1},{3,2},{4,7},{5,4},{6,5},{7,6},{8,11},{9,8},{10,9... | collective-permute-start | bytes 393224 | tf_op jit(solution)/shard_map/ppermute | solution.py:179
  135.5 10.4 %collective-permute-start.18 = (bf16[128,512]{1,0:T(8,128)(2,1)S(1)}, bf16[128,512]{1,0:T(8,128)(2,1)S(1)}, u32[]{:S(2)}, u32[]{:S(2)}) collective-permute-start(bf16[128,512]{1,0:T(8,128)(2,1)S(1)} %get-tuple-element.42), channel_id=1, source_target_pairs={{0,1},{1,2},{2,3},{3,0},{4,5},{5,6},{6,7},{7,4},{8,9},{9,10},{10,1... | collective-permute-start | bytes 393224 | tf_op jit(solution)/shard_map/ppermute | solution.py:179
  135.5 12.9 %collective-permute-start.17 = (bf16[128,512]{1,0:T(8,128)(2,1)S(1)}, bf16[128,512]{1,0:T(8,128)(2,1)S(1)}, u32[]{:S(2)}, u32[]{:S(2)}) collective-permute-start(bf16[128,512]{1,0:T(8,128)(2,1)S(1)} %get-tuple-element.43), channel_id=1, source_target_pairs={{0,2},{1,3},{2,0},{3,1},{4,6},{5,7},{6,4},{7,5},{8,10},{9,11},{10,... | collective-permute-start | bytes 393224 | tf_op jit(solution)/shard_map/ppermute | solution.py:179
  137.8 12.5 %collective-permute-start.22 = (bf16[128,512]{1,0:T(8,128)(2,1)}, bf16[128,512]{1,0:T(8,128)(2,1)S(1)}, u32[]{:S(2)}, u32[]{:S(2)}) collective-permute-start(bf16[128,512]{1,0:T(8,128)(2,1)} %get-tuple-element.32), channel_id=1, source_target_pairs={{0,12},{4,0},{8,4},{12,8},{1,13},{5,1},{9,5},{13,9},{2,14},{6,2},{... | collective-permute-start | bytes 393224 | tf_op jit(solution)/shard_map/ppermute | solution.py:179
  140.5 9.8 %collective-permute-start.23 = (bf16[128,512]{1,0:T(8,128)(2,1)S(1)}, bf16[128,512]{1,0:T(8,128)(2,1)S(1)}, u32[]{:S(2)}, u32[]{:S(2)}) collective-permute-start(bf16[128,512]{1,0:T(8,128)(2,1)S(1)} %get-tuple-element.33), channel_id=1, source_target_pairs={{0,8},{4,12},{8,0},{12,4},{1,9},{5,13},{9,1},{13,5},{2,10},{6,14},... | collective-permute-start | bytes 393224 | tf_op jit(solution)/shard_map/ppermute | solution.py:179
  145.8 6.2 %collective-permute-start.24 = (bf16[128,512]{1,0:T(8,128)(2,1)S(1)}, bf16[128,512]{1,0:T(8,128)(2,1)S(1)}, u32[]{:S(2)}, u32[]{:S(2)}) collective-permute-start(bf16[128,512]{1,0:T(8,128)(2,1)S(1)} %get-tuple-element.34), channel_id=1, source_target_pairs={{0,4},{4,8},{8,12},{12,0},{1,5},{5,9},{9,13},{13,1},{2,6},{6,10},{... | collective-permute-start | bytes 393224 | tf_op jit(solution)/shard_map/ppermute | solution.py:179
  (13 other events, 190.2 us)
Sparse Core Ops, SparseCore 0:
  10.7 55.9 all-gather.2
  82.2 41.7 reduce-scatter.1

commit v2 on v0

--- a/solution.py
+++ b/solution.py
@@ -174,10 +174,6 @@
     wait_all(send_parts(acc, stage, outs, sems, count, per, projections[0] == 2))
 
 
-def pair_kernel(a, b, out, sems):
-    wait_all(start_all([(a, out.at[0]), (b, out.at[1])], sems, 0))
-
-
 def shift(value, axis, hop):
     size = lax.axis_size(axis)
     return lax.ppermute(value, axis, [(i, (i + hop) % size) for i in range(size)])
@@ -203,7 +199,9 @@
 
 def collect(outs, grads):
     ring = len(outs)
-    first = [[p[0]] + [shift(p[h], a, -h) for h in range(1, ring)] for p, a in ((outs, "x"), (grads, "z"))]
+    first = []
+    for p, a in ((outs, "x"), (grads, "z")):
+        first.append([p[0]] + [shift(p[h], a, -h) for h in range(1, ring)])
     done = []
     for terms, axis in zip(first, ("z", "x")):
         sums = [total(*[t[turn] for t in terms]) for turn in range(ring)]
@@ -236,15 +234,7 @@
     count = 3 * held
     tok = tokens.shape[0]
 
-    pair = pl.pallas_call(
-        pair_kernel,
-        out_shape=jax.ShapeDtypeStruct((2,) + tokens.shape, BF),
-        in_specs=[ANY] * 2,
-        out_specs=ANY,
-        scratch_shapes=[pltpu.SemaphoreType.DMA((2,))],
-        name="pair",
-    )(tokens, grad_out)
-    x_all = lax.all_gather(pair, MP, axis=0, tiled=False)
+    x_all = lax.all_gather(jnp.stack([tokens, grad_out]), MP, axis=0, tiled=False)
 
     slabs = jnp.stack(
         [

time: 165 us -> 158 us (0.958)
  Pallas kernels: 31.1 us -> 22 us
  other arithmetic: 9.86 us -> 11.7 us
    pallas_call x1 -> x0, Pallas kernels: 9.06 us -> none  [body(): pl.pallas_call(pair_kernel, out_shape=jax.ShapeDtypeStruct((2,) + tokens....]
    another operation x0 -> x1, other arithmetic: none -> 1.84 us  [body(): jnp.stack([tokens, grad_out])]
where the time goes in v2:
time: 158 us; the launch traced here: 157 us
  waiting for transfers between devices  41.1 us (26%)
  starting transfers between devices  35.3 us (22%)
  blocking collectives  23.7 us (15%)
  Pallas kernels  22 us (14%)
  between operations  14.3 us (9%)
  other arithmetic  11.7 us (7%)
  local copies, waits for them, and re-layouts  8.89 us (6%)
    ppermute x25, waiting for transfers between devices, shift(): lax.ppermute(value, axis, [(i, (i + hop) % size) for i in range(size)])  32.3 us
    ppermute x25, starting transfers between devices, shift(): lax.ppermute(value, axis, [(i, (i + hop) % size) for i in range(size)])  28.5 us
    all_to_all x1, blocking collectives, body(): mine = lax.all_to_all(slabs, MP, split_axis=0, concat_axis=0, tiled=True)  23.7 us
    pallas_call x1, Pallas kernels, body(): pl.pallas_call(functools.partial(owner_kernel, owned=owned, **sizes), out...  14.2 us
    reduce_scatter x1, waiting for transfers between devices, body(): grads = lax.psum_scatter(grads, DP, scatter_dimension=0, tiled=True)  8.79 us
    pallas_call x1, Pallas kernels, parts_of(): pl.pallas_call(functools.partial(parts_kernel, projections=projections, *...  7.87 us
    all_to_all x1, starting transfers between devices, body(): grads = lax.all_to_all(grads, MP, split_axis=0, concat_axis=0, tiled=True)  6.76 us
    another operation x6, local copies, waits for them, and re-layouts, body(): tables = jnp.stack([gate_block_pairs, up_blocks, down_blocks])  4.24 us
  transfers between devices with their start and end apart: 28, of which 10 were waited for; matrix products, arithmetic and copies ran while one was open for 11% of the time, Pallas kernels for 5%

profile of v2, /device:TPU:0, one launch (start us, length us, event | category | flops | bytes accessed | tf_op | source)
XLA Modules:
  0.0 157.0 jit_solution(8471694675100430856)
XLA Ops:
  7.2 1.8 %pad_maximum_fusion.1 = bf16[2,128,512]{2,1,0:T(8,128)(2,1)} fusion(bf16[1,128,512]{2,1,0:T(8,128)(2,1)} %bitcast.88, bf16[1,128,512]{2,1,0:T(8,128)(2,1)} %bitcast.89), kind=kLoop, calls=%fused_computation.1 | loop fusion | flops 131072 | bytes 524288 | tf_op jit(solution)/shard_map/stack | solution.py:237
  10.4 23.7 %all_to_all.10.refs_0_ = bf16[16,3,4,16,128]{4,3,2,1,0:T(8,128)(2,1)S(1)} all-to-all(bf16[16,3,4,16,128]{4,3,2,1,0:T(8,128)(2,1)S(1)} %pad_maximum_fusion), channel_id=1, replica_groups=mesh['y'=4,'c'=2,'x'=4,'z'=4] {'x','z'}, dimensions={0} | all-to-all | bytes 1572864 | tf_op jit(solution)/shard_map/all_to_all | solution.py:246
  35.1 3.1 %collective-permute-start.5 = (bf16[96,16,128]{2,1,0:T(8,128)(2,1)S(1)}, bf16[96,16,128]{2,1,0:T(8,128)(2,1)S(1)}, u32[]{:S(2)}, u32[]{:S(2)}) collective-permute-start(bf16[96,16,128]{2,1,0:T(8,128)(2,1)S(1)} %bitcast.83), channel_id=1, source_target_pairs={{0,96},{32,0},{64,32},{96,64},{1,97},{33,1},{65,33},{97,65},{2,98}... | collective-permute-start | bytes 1179656 | tf_op jit(solution)/shard_map/ppermute | solution.py:179
  38.2 3.2 %collective-permute-start.6 = (bf16[96,16,128]{2,1,0:T(8,128)(2,1)}, bf16[96,16,128]{2,1,0:T(8,128)(2,1)}, u32[]{:S(2)}, u32[]{:S(2)}) collective-permute-start(bf16[96,16,128]{2,1,0:T(8,128)(2,1)} %bitcast.19), channel_id=1, source_target_pairs={{0,96},{32,0},{64,32},{96,64},{1,97},{33,1},{65,33},{97,65},{2,98}... | collective-permute-start | bytes 1179656 | tf_op jit(solution)/shard_map/ppermute | solution.py:179
  41.4 6.3 %collective-permute-done.5.refs_6_ = bf16[96,16,128]{2,1,0:T(8,128)(2,1)S(1)} collective-permute-done((bf16[96,16,128]{2,1,0:T(8,128)(2,1)S(1)}, bf16[96,16,128]{2,1,0:T(8,128)(2,1)S(1)}, u32[]{:S(2)}, u32[]{:S(2)}) %collective-permute-start.5) | collective-permute-done | bytes 393248 | tf_op jit(solution)/shard_map/ppermute | solution.py:179
  47.7 3.8 %collective-permute-done.1.refs_2_ = bf16[96,16,128]{2,1,0:T(8,128)(2,1)} collective-permute-done((bf16[96,16,128]{2,1,0:T(8,128)(2,1)S(1)}, bf16[96,16,128]{2,1,0:T(8,128)(2,1)}, u32[]{:S(2)}, u32[]{:S(2)}) %collective-permute-start.1) | collective-permute-done | bytes 393248 | tf_op jit(solution)/shard_map/ppermute | solution.py:179
  52.5 3.7 %collective-permute-start.10 = (bf16[96,16,128]{2,1,0:T(8,128)(2,1)}, bf16[96,16,128]{2,1,0:T(8,128)(2,1)}, u32[]{:S(2)}, u32[]{:S(2)}) collective-permute-start(bf16[96,16,128]{2,1,0:T(8,128)(2,1)} %collective-permute-done.6.refs_7_), channel_id=1, source_target_pairs={{0,96},{32,0},{64,32},{96,64},{1,97},{33,1},{65,33},{97,65},{2,98}... | collective-permute-start | bytes 1179656 | tf_op jit(solution)/shard_map/ppermute | solution.py:179
  62.3 2.0 %collective-permute-done.9.refs_10_ = bf16[96,16,128]{2,1,0:T(8,128)(2,1)} collective-permute-done((bf16[96,16,128]{2,1,0:T(8,128)(2,1)}, bf16[96,16,128]{2,1,0:T(8,128)(2,1)}, u32[]{:S(2)}, u32[]{:S(2)}) %collective-permute-start.9) | collective-permute-done | bytes 393248 | tf_op jit(solution)/shard_map/ppermute | solution.py:179
  67.7 14.2 %owner.1 = (bf16[3,7,128,128]{3,2,1,0:T(8,128)(2,1)}, bf16[128,896]{1,0:T(8,128)(2,1)}, bf16[8,192,16,128]{3,2,1,0:T(8,128)(2,1)}, bf16[4,128,512]{2,1,0:T(8,128...) custom-call(s32[192]{0:T(256)} %get-tuple-element.29.rows, ...), custom_call_target="tpu_custom_call" | custom-call | tf_op jit(solution)/shard_map/owner/pallas_call | solution.py:273
  81.9 2.2 %collective-permute-start.13 = (bf16[4,128,512]{2,1,0:T(8,128)(2,1)}, bf16[4,128,512]{2,1,0:T(8,128)(2,1)S(1)}, u32[]{:S(2)}, u32[]{:S(2)}) collective-permute-start(bf16[4,128,512]{2,1,0:T(8,128)(2,1)} %get-tuple-element.19), channel_id=1, source_target_pairs={{0,12},{4,0},{8,4},{12,8},{1,13},{5,1},{9,5},{13,9},{2,14},{6,2},{... | collective-permute-start | bytes 1572872 | tf_op jit(solution)/shard_map/ppermute | solution.py:179
  85.3 7.9 %shard_map.136 = (bf16[4,128,512]{2,1,0:T(8,128)(2,1)}, bf16[4,128,512]{2,1,0:T(8,128)(2,1)}, bf16[4,128,512]{2,1,0:T(8,128)(2,1)}, bf16[4,128,512]{2,1,0:T(8,128)(2,1)}) custom-call(s32[192]{0:T(256)} %get-tuple-element.28.hops.rows, s32[192]{0:T(256)} %select_reduce_fusion.cols, s32[8]{0:T(128)} %stack.63.slots, ...), custom_call_target="tpu_custom_call" | custom-call | tf_op jit(solution)/shard_map/pallas_call | solution.py:299
  95.8 11.6 %collective-permute-done.13 = bf16[4,128,512]{2,1,0:T(8,128)(2,1)S(1)} collective-permute-done((bf16[4,128,512]{2,1,0:T(8,128)(2,1)}, bf16[4,128,512]{2,1,0:T(8,128)(2,1)S(1)}, u32[]{:S(2)}, u32[]{:S(2)}) %collective-permute-start.13) | collective-permute-done | bytes 524320 | tf_op jit(solution)/shard_map/ppermute | solution.py:179
  108.0 3.0 %collective-permute-done.15 = bf16[4,128,512]{2,1,0:T(8,128)(2,1)} collective-permute-done((bf16[4,128,512]{2,1,0:T(8,128)(2,1)}, bf16[4,128,512]{2,1,0:T(8,128)(2,1)}, u32[]{:S(2)}, u32[]{:S(2)}) %collective-permute-start.15) | collective-permute-done | bytes 524320 | tf_op jit(solution)/shard_map/ppermute | solution.py:179
  111.0 2.1 %fusion.6 = (bf16[128,512]{1,0:T(8,128)(2,1)}, bf16[128,512]{1,0:T(8,128)(2,1)}, bf16[128,512]{1,0:T(8,128)(2,1)S(1)}) fusion(bf16[4,128,512]{2,1,0:T(8,128)(2,1)} %collective-permute-done.15, bf16[4,128,512]{2,1,0:T(8,128)(2,1)} %collective-permute-done.14, bf16[4,128,512]{2,1,0:T(8,128)(2,1)S(1)} %collective-permute-done.13, ...), kind=kLoop, calls=%fused_computation.18 | loop fusion | flops 1572864 | bytes 1966080 | tf_op jit(solution)/shard_map/add | solution.py:183
  113.6 1.6 %collective-permute-start.18 = (bf16[128,512]{1,0:T(8,128)(2,1)}, bf16[128,512]{1,0:T(8,128)(2,1)S(1)}, u32[]{:S(2)}, u32[]{:S(2)}) collective-permute-start(bf16[128,512]{1,0:T(8,128)(2,1)} %get-tuple-element.34), channel_id=1, source_target_pairs={{0,1},{1,2},{2,3},{3,0},{4,5},{5,6},{6,7},{7,4},{8,9},{9,10},{10,1... | collective-permute-start | bytes 393224 | tf_op jit(solution)/shard_map/ppermute | solution.py:179
  115.2 8.8 %reduce-scatter.2.cloned.1.call-done = bf16[1,192,16,128]{3,2,1,0:T(8,128)(2,1)} async-done(((bf16[8,192,16,128]{3,2,1,0:T(8,128)(2,1)}), bf16[1,192,16,128]{3,2,1,0:T(8,128)(2,1)}) %reduce-scatter.2.cloned.1.call-update) | async-done | bytes 786448 | tf_op jit(solution)/shard_map/reduce_scatter | solution.py:294
  124.0 6.8 %all-to-all-start.1 = ((bf16[16,3,4,16,128]{4,3,2,1,0:T(8,128)(2,1)}), bf16[16,3,4,16,128]{4,3,2,1,0:T(8,128)(2,1)S(1)}, u32[]{:S(2)}, u32[]{:S(2)}) async-start(bf16[16,3,4,16,128]{4,3,2,1,0:T(8,128)(2,1)} %bitcast.82), calls=%async_computation.2 | async-start | bytes 1572864 | tf_op jit(solution)/shard_map/all_to_all | solution.py:315
  130.7 3.5 %collective-permute-start.17 = (bf16[128,512]{1,0:T(8,128)(2,1)S(1)}, bf16[128,512]{1,0:T(8,128)(2,1)S(1)}, u32[]{:S(2)}, u32[]{:S(2)}) collective-permute-start(bf16[128,512]{1,0:T(8,128)(2,1)S(1)} %get-tuple-element.35), channel_id=1, source_target_pairs={{0,2},{1,3},{2,0},{3,1},{4,6},{5,7},{6,4},{7,5},{8,10},{9,11},{10,... | collective-permute-start | bytes 393224 | tf_op jit(solution)/shard_map/ppermute | solution.py:179
  134.3 1.6 %fusion.9 = (bf16[128,512]{1,0:T(8,128)(2,1)S(1)}, bf16[128,512]{1,0:T(8,128)(2,1)S(1)}, bf16[128,512]{1,0:T(8,128)(2,1)S(1)}) fusion(bf16[4,128,512]{2,1,0:T(8,128)(2,1)} %collective-permute-done.21, bf16[4,128,512]{2,1,0:T(8,128)(2,1)} %collective-permute-done.20, bf16[4,128,512]{2,1,0:T(8,128)(2,1)} %collective-permute-done.19, ...), kind=kLoop, calls=%fused_computation.21 | loop fusion | flops 1572864 | bytes 1966080 | tf_op jit(solution)/shard_map/add | solution.py:183
  135.9 2.7 %collective-permute-start.22 = (bf16[128,512]{1,0:T(8,128)(2,1)S(1)}, bf16[128,512]{1,0:T(8,128)(2,1)S(1)}, u32[]{:S(2)}, u32[]{:S(2)}) collective-permute-start(bf16[128,512]{1,0:T(8,128)(2,1)S(1)} %get-tuple-element.30), channel_id=1, source_target_pairs={{0,12},{4,0},{8,4},{12,8},{1,13},{5,1},{9,5},{13,9},{2,14},{6,2},{... | collective-permute-start | bytes 393224 | tf_op jit(solution)/shard_map/ppermute | solution.py:179
  138.7 2.3 %collective-permute-start.23 = (bf16[128,512]{1,0:T(8,128)(2,1)S(1)}, bf16[128,512]{1,0:T(8,128)(2,1)S(1)}, u32[]{:S(2)}, u32[]{:S(2)}) collective-permute-start(bf16[128,512]{1,0:T(8,128)(2,1)S(1)} %get-tuple-element.32), channel_id=1, source_target_pairs={{0,8},{4,12},{8,0},{12,4},{1,9},{5,13},{9,1},{13,5},{2,10},{6,14},... | collective-permute-start | bytes 393224 | tf_op jit(solution)/shard_map/ppermute | solution.py:179
  141.0 2.2 %collective-permute-done.17 = bf16[128,512]{1,0:T(8,128)(2,1)S(1)} collective-permute-done((bf16[128,512]{1,0:T(8,128)(2,1)S(1)}, bf16[128,512]{1,0:T(8,128)(2,1)S(1)}, u32[]{:S(2)}, u32[]{:S(2)}) %collective-permute-start.17) | collective-permute-done | bytes 131104 | tf_op jit(solution)/shard_map/ppermute | solution.py:179
  143.1 1.9 %fusion.5 = bf16[128,512]{1,0:T(8,128)(2,1)} fusion(bf16[128,512]{1,0:T(8,128)(2,1)S(1)} %collective-permute-done.18, bf16[128,512]{1,0:T(8,128)(2,1)S(1)} %collective-permute-done.17, bf16[128,512]{1,0:T(8,128)(2,1)S(1)} %collective-permute-done.16, bf16[4,128,512]{2,1,0:T(8,128)(2,1)} %collective-permute-done.15, ...), kind=kLoop, calls=%fused_computation.9 | loop fusion | flops 917504 | bytes 1048576 | tf_op jit(solution)/shard_map/convert_element_type | solution.py:209
  147.4 1.9 %fusion.2 = bf16[128,512]{1,0:T(8,128)(2,1)} fusion(bf16[128,512]{1,0:T(8,128)(2,1)S(1)} %collective-permute-done.24, bf16[128,512]{1,0:T(8,128)(2,1)S(1)} %collective-permute-done.23, bf16[128,512]{1,0:T(8,128)(2,1)S(1)} %collective-permute-done.22, bf16[4,128,512]{2,1,0:T(8,128)(2,1)} %collective-permute-done.21, ...), kind=kLoop, calls=%fused_computation.5 | loop fusion | flops 917504 | bytes 1048576 | tf_op jit(solution)/shard_map/convert_element_type | solution.py:209
  (83 shorter events, 20.8 us)
Async XLA Ops:
  7.2 60.5 %all-gather.3.cloned.1.call-start = ((), (), s32[]{:S(2)}) async-start(), calls=%async_computation.4 | async-start | bytes 4456448 | tf_op jit(solution)/shard_map/all_gather | solution.py:237
  9.1 114.9 %reduce-scatter.2.cloned.1.call-start = ((), (), s32[]{:S(2)}) async-start(), calls=%async_computation.3 | async-start | bytes 7077888 | tf_op jit(solution)/shard_map/reduce_scatter | solution.py:294
  35.1 12.6 %collective-permute-start.5 = (bf16[96,16,128]{2,1,0:T(8,128)(2,1)S(1)}, bf16[96,16,128]{2,1,0:T(8,128)(2,1)S(1)}, u32[]{:S(2)}, u32[]{:S(2)}) collective-permute-start(bf16[96,16,128]{2,1,0:T(8,128)(2,1)S(1)} %bitcast.83), channel_id=1, source_target_pairs={{0,96},{32,0},{64,32},{96,64},{1,97},{33,1},{65,33},{97,65},{2,98}... | collective-permute-start | bytes 1179656 | tf_op jit(solution)/shard_map/ppermute | solution.py:179
  38.2 13.3 %collective-permute-start.1 = (bf16[96,16,128]{2,1,0:T(8,128)(2,1)S(1)}, bf16[96,16,128]{2,1,0:T(8,128)(2,1)}, u32[]{:S(2)}, u32[]{:S(2)}) collective-permute-start(bf16[96,16,128]{2,1,0:T(8,128)(2,1)S(1)} %bitcast.84), channel_id=1, source_target_pairs={{0,32},{32,64},{64,96},{96,0},{1,33},{33,65},{65,97},{97,1},{2,34}... | collective-permute-start | bytes 1179656 | tf_op jit(solution)/shard_map/ppermute | solution.py:179
  38.2 14.3 %collective-permute-start.6 = (bf16[96,16,128]{2,1,0:T(8,128)(2,1)}, bf16[96,16,128]{2,1,0:T(8,128)(2,1)}, u32[]{:S(2)}, u32[]{:S(2)}) collective-permute-start(bf16[96,16,128]{2,1,0:T(8,128)(2,1)} %bitcast.19), channel_id=1, source_target_pairs={{0,96},{32,0},{64,32},{96,64},{1,97},{33,1},{65,33},{97,65},{2,98}... | collective-permute-start | bytes 1179656 | tf_op jit(solution)/shard_map/ppermute | solution.py:179
  41.4 19.1 %collective-permute-start.2 = (bf16[96,16,128]{2,1,0:T(8,128)(2,1)}, bf16[96,16,128]{2,1,0:T(8,128)(2,1)}, u32[]{:S(2)}, u32[]{:S(2)}) collective-permute-start(bf16[96,16,128]{2,1,0:T(8,128)(2,1)} %bitcast.19), channel_id=1, source_target_pairs={{0,32},{32,64},{64,96},{96,0},{1,33},{33,65},{65,97},{97,1},{2,34}... | collective-permute-start | bytes 1179656 | tf_op jit(solution)/shard_map/ppermute | solution.py:179
  47.7 14.0 %collective-permute-start.7 = (bf16[96,16,128]{2,1,0:T(8,128)(2,1)S(1)}, bf16[96,16,128]{2,1,0:T(8,128)(2,1)}, u32[]{:S(2)}, u32[]{:S(2)}) collective-permute-start(bf16[96,16,128]{2,1,0:T(8,128)(2,1)S(1)} %collective-permute-done.5.refs_6_), channel_id=1, source_target_pairs={{0,16},{16,0},{1,17},{17,1},{2,18},{18,2},{3,19},{19,3},{4,20},{20... | collective-permute-start | bytes 1179656 | tf_op jit(solution)/shard_map/ppermute | solution.py:179
  51.5 12.8 %collective-permute-start.9 = (bf16[96,16,128]{2,1,0:T(8,128)(2,1)}, bf16[96,16,128]{2,1,0:T(8,128)(2,1)}, u32[]{:S(2)}, u32[]{:S(2)}) collective-permute-start(bf16[96,16,128]{2,1,0:T(8,128)(2,1)} %collective-permute-done.1.refs_2_), channel_id=1, source_target_pairs={{0,32},{32,64},{64,96},{96,0},{1,33},{33,65},{65,97},{97,1},{2,34}... | collective-permute-start | bytes 1179656 | tf_op jit(solution)/shard_map/ppermute | solution.py:179
  51.5 12.9 %collective-permute-start.3 = (bf16[96,16,128]{2,1,0:T(8,128)(2,1)}, bf16[96,16,128]{2,1,0:T(8,128)(2,1)}, u32[]{:S(2)}, u32[]{:S(2)}) collective-permute-start(bf16[96,16,128]{2,1,0:T(8,128)(2,1)} %collective-permute-done.1.refs_2_), channel_id=1, source_target_pairs={{0,16},{16,0},{1,17},{17,1},{2,18},{18,2},{3,19},{19,3},{4,20},{20... | collective-permute-start | bytes 1179656 | tf_op jit(solution)/shard_map/ppermute | solution.py:179
  52.5 12.4 %collective-permute-start.10 = (bf16[96,16,128]{2,1,0:T(8,128)(2,1)}, bf16[96,16,128]{2,1,0:T(8,128)(2,1)}, u32[]{:S(2)}, u32[]{:S(2)}) collective-permute-start(bf16[96,16,128]{2,1,0:T(8,128)(2,1)} %collective-permute-done.6.refs_7_), channel_id=1, source_target_pairs={{0,96},{32,0},{64,32},{96,64},{1,97},{33,1},{65,33},{97,65},{2,98}... | collective-permute-start | bytes 1179656 | tf_op jit(solution)/shard_map/ppermute | solution.py:179
  60.5 7.1 %collective-permute-start = (bf16[192,16,128]{2,1,0:T(8,128)(2,1)S(1)}, bf16[192,16,128]{2,1,0:T(8,128)(2,1)}, u32[]{:S(2)}, u32[]{:S(2)}) collective-permute-start(bf16[192,16,128]{2,1,0:T(8,128)(2,1)S(1)} %bitcast.75), channel_id=1, source_target_pairs={{0,16},{16,0},{1,17},{17,1},{2,18},{18,2},{3,19},{19,3},{4,20},{20... | collective-permute-start | bytes 2359304 | tf_op jit(solution)/shard_map/ppermute | solution.py:179
  81.9 25.6 %collective-permute-start.13 = (bf16[4,128,512]{2,1,0:T(8,128)(2,1)}, bf16[4,128,512]{2,1,0:T(8,128)(2,1)S(1)}, u32[]{:S(2)}, u32[]{:S(2)}) collective-permute-start(bf16[4,128,512]{2,1,0:T(8,128)(2,1)} %get-tuple-element.19), channel_id=1, source_target_pairs={{0,12},{4,0},{8,4},{12,8},{1,13},{5,1},{9,5},{13,9},{2,14},{6,2},{... | collective-permute-start | bytes 1572872 | tf_op jit(solution)/shard_map/ppermute | solution.py:179
  84.1 23.9 %collective-permute-start.14 = (bf16[4,128,512]{2,1,0:T(8,128)(2,1)}, bf16[4,128,512]{2,1,0:T(8,128)(2,1)}, u32[]{:S(2)}, u32[]{:S(2)}) collective-permute-start(bf16[4,128,512]{2,1,0:T(8,128)(2,1)} %get-tuple-element.20), channel_id=1, source_target_pairs={{0,8},{4,12},{8,0},{12,4},{1,9},{5,13},{9,1},{13,5},{2,10},{6,14},... | collective-permute-start | bytes 1572872 | tf_op jit(solution)/shard_map/ppermute | solution.py:179
  84.6 26.5 %collective-permute-start.15 = (bf16[4,128,512]{2,1,0:T(8,128)(2,1)}, bf16[4,128,512]{2,1,0:T(8,128)(2,1)}, u32[]{:S(2)}, u32[]{:S(2)}) collective-permute-start(bf16[4,128,512]{2,1,0:T(8,128)(2,1)} %get-tuple-element.21), channel_id=1, source_target_pairs={{0,4},{4,8},{8,12},{12,0},{1,5},{5,9},{9,13},{13,1},{2,6},{6,10},{... | collective-permute-start | bytes 1572872 | tf_op jit(solution)/shard_map/ppermute | solution.py:179
  93.2 37.6 %collective-permute-start.19 = (bf16[4,128,512]{2,1,0:T(8,128)(2,1)}, bf16[4,128,512]{2,1,0:T(8,128)(2,1)}, u32[]{:S(2)}, u32[]{:S(2)}) collective-permute-start(bf16[4,128,512]{2,1,0:T(8,128)(2,1)} %get-tuple-element.24), channel_id=1, source_target_pairs={{0,3},{1,0},{2,1},{3,2},{4,7},{5,4},{6,5},{7,6},{8,11},{9,8},{10,9... | collective-permute-start | bytes 1572872 | tf_op jit(solution)/shard_map/ppermute | solution.py:179
  94.7 39.6 %collective-permute-start.20 = (bf16[4,128,512]{2,1,0:T(8,128)(2,1)}, bf16[4,128,512]{2,1,0:T(8,128)(2,1)}, u32[]{:S(2)}, u32[]{:S(2)}) collective-permute-start(bf16[4,128,512]{2,1,0:T(8,128)(2,1)} %get-tuple-element.25), channel_id=1, source_target_pairs={{0,2},{1,3},{2,0},{3,1},{4,6},{5,7},{6,4},{7,5},{8,10},{9,11},{10,... | collective-permute-start | bytes 1572872 | tf_op jit(solution)/shard_map/ppermute | solution.py:179
  107.4 26.8 %collective-permute-start.21 = (bf16[4,128,512]{2,1,0:T(8,128)(2,1)}, bf16[4,128,512]{2,1,0:T(8,128)(2,1)}, u32[]{:S(2)}, u32[]{:S(2)}) collective-permute-start(bf16[4,128,512]{2,1,0:T(8,128)(2,1)} %get-tuple-element.26), channel_id=1, source_target_pairs={{0,1},{1,2},{2,3},{3,0},{4,5},{5,6},{6,7},{7,4},{8,9},{9,10},{10,1... | collective-permute-start | bytes 1572872 | tf_op jit(solution)/shard_map/ppermute | solution.py:179
  113.1 25.5 %collective-permute-start.16 = (bf16[128,512]{1,0:T(8,128)(2,1)}, bf16[128,512]{1,0:T(8,128)(2,1)S(1)}, u32[]{:S(2)}, u32[]{:S(2)}) collective-permute-start(bf16[128,512]{1,0:T(8,128)(2,1)} %get-tuple-element.33), channel_id=1, source_target_pairs={{0,3},{1,0},{2,1},{3,2},{4,7},{5,4},{6,5},{7,6},{8,11},{9,8},{10,9... | collective-permute-start | bytes 393224 | tf_op jit(solution)/shard_map/ppermute | solution.py:179
  113.6 27.4 %collective-permute-start.18 = (bf16[128,512]{1,0:T(8,128)(2,1)}, bf16[128,512]{1,0:T(8,128)(2,1)S(1)}, u32[]{:S(2)}, u32[]{:S(2)}) collective-permute-start(bf16[128,512]{1,0:T(8,128)(2,1)} %get-tuple-element.34), channel_id=1, source_target_pairs={{0,1},{1,2},{2,3},{3,0},{4,5},{5,6},{6,7},{7,4},{8,9},{9,10},{10,1... | collective-permute-start | bytes 393224 | tf_op jit(solution)/shard_map/ppermute | solution.py:179
  124.0 25.3 %all-to-all-start.1 = ((bf16[16,3,4,16,128]{4,3,2,1,0:T(8,128)(2,1)}), bf16[16,3,4,16,128]{4,3,2,1,0:T(8,128)(2,1)S(1)}, u32[]{:S(2)}, u32[]{:S(2)}) async-start(bf16[16,3,4,16,128]{4,3,2,1,0:T(8,128)(2,1)} %bitcast.82), calls=%async_computation.2 | async-start | bytes 1572864 | tf_op jit(solution)/shard_map/all_to_all | solution.py:315
  130.7 12.4 %collective-permute-start.17 = (bf16[128,512]{1,0:T(8,128)(2,1)S(1)}, bf16[128,512]{1,0:T(8,128)(2,1)S(1)}, u32[]{:S(2)}, u32[]{:S(2)}) collective-permute-start(bf16[128,512]{1,0:T(8,128)(2,1)S(1)} %get-tuple-element.35), channel_id=1, source_target_pairs={{0,2},{1,3},{2,0},{3,1},{4,6},{5,7},{6,4},{7,5},{8,10},{9,11},{10,... | collective-permute-start | bytes 393224 | tf_op jit(solution)/shard_map/ppermute | solution.py:179
  135.9 9.1 %collective-permute-start.22 = (bf16[128,512]{1,0:T(8,128)(2,1)S(1)}, bf16[128,512]{1,0:T(8,128)(2,1)S(1)}, u32[]{:S(2)}, u32[]{:S(2)}) collective-permute-start(bf16[128,512]{1,0:T(8,128)(2,1)S(1)} %get-tuple-element.30), channel_id=1, source_target_pairs={{0,12},{4,0},{8,4},{12,8},{1,13},{5,1},{9,5},{13,9},{2,14},{6,2},{... | collective-permute-start | bytes 393224 | tf_op jit(solution)/shard_map/ppermute | solution.py:179
  138.6 7.3 %collective-permute-start.24 = (bf16[128,512]{1,0:T(8,128)(2,1)S(1)}, bf16[128,512]{1,0:T(8,128)(2,1)S(1)}, u32[]{:S(2)}, u32[]{:S(2)}) collective-permute-start(bf16[128,512]{1,0:T(8,128)(2,1)S(1)} %get-tuple-element.31), channel_id=1, source_target_pairs={{0,4},{4,8},{8,12},{12,0},{1,5},{5,9},{9,13},{13,1},{2,6},{6,10},{... | collective-permute-start | bytes 393224 | tf_op jit(solution)/shard_map/ppermute | solution.py:179
  138.7 8.7 %collective-permute-start.23 = (bf16[128,512]{1,0:T(8,128)(2,1)S(1)}, bf16[128,512]{1,0:T(8,128)(2,1)S(1)}, u32[]{:S(2)}, u32[]{:S(2)}) collective-permute-start(bf16[128,512]{1,0:T(8,128)(2,1)S(1)} %get-tuple-element.32), channel_id=1, source_target_pairs={{0,8},{4,12},{8,0},{12,4},{1,9},{5,13},{9,1},{13,5},{2,10},{6,14},... | collective-permute-start | bytes 393224 | tf_op jit(solution)/shard_map/ppermute | solution.py:179
  (12 other events, 212.4 us)
Sparse Core Ops, SparseCore 0:
  10.7 55.9 all-gather.2
  82.0 41.9 reduce-scatter.1

commit v3 on v2

--- a/solution.py
+++ b/solution.py
@@ -8,7 +8,7 @@
 from jax.sharding import Mesh, PartitionSpec as P
 
 BS = 128
-UNROLL = 4
+UNROLL = 8
 MP = ("x", "z")
 DP = ("y", "c")
 BF = jnp.bfloat16
@@ -199,9 +199,7 @@
 
 def collect(outs, grads):
     ring = len(outs)
-    first = []
-    for p, a in ((outs, "x"), (grads, "z")):
-        first.append([p[0]] + [shift(p[h], a, -h) for h in range(1, ring)])
+    first = [[p[0]] + [shift(p[h], a, -h) for h in range(1, ring)] for p, a in ((outs, "x"), (grads, "z"))]
     done = []
     for terms, axis in zip(first, ("z", "x")):
         sums = [total(*[t[turn] for t in terms]) for turn in range(ring)]

time: 158 us -> 159 us (level)
  no operation moved by 1% of the time
where the time goes in v3:
time: 159 us; the launch traced here: 158 us
  waiting for transfers between devices  41.4 us (26%)
  starting transfers between devices  35.3 us (22%)
  blocking collectives  23.7 us (15%)
  Pallas kernels  23 us (14%)
  between operations  14.3 us (9%)
  other arithmetic  11.7 us (7%)
  local copies, waits for them, and re-layouts  8.89 us (6%)
    ppermute x25, waiting for transfers between devices, shift(): lax.ppermute(value, axis, [(i, (i + hop) % size) for i in range(size)])  32.7 us
    ppermute x25, starting transfers between devices, shift(): lax.ppermute(value, axis, [(i, (i + hop) % size) for i in range(size)])  28.4 us
    all_to_all x1, blocking collectives, body(): mine = lax.all_to_all(slabs, MP, split_axis=0, concat_axis=0, tiled=True)  23.7 us
    pallas_call x1, Pallas kernels, body(): pl.pallas_call(functools.partial(owner_kernel, owned=owned, **sizes), out...  15.4 us
    reduce_scatter x1, waiting for transfers between devices, body(): grads = lax.psum_scatter(grads, DP, scatter_dimension=0, tiled=True)  8.61 us
    pallas_call x1, Pallas kernels, parts_of(): pl.pallas_call(functools.partial(parts_kernel, projections=projections, *...  7.62 us
    all_to_all x1, starting transfers between devices, body(): grads = lax.all_to_all(grads, MP, split_axis=0, concat_axis=0, tiled=True)  6.78 us
    another operation x6, local copies, waits for them, and re-layouts, body(): tables = jnp.stack([gate_block_pairs, up_blocks, down_blocks])  4.24 us
  transfers between devices with their start and end apart: 28, of which 10 were waited for; matrix products, arithmetic and copies ran while one was open for 11% of the time, Pallas kernels for 5%

profile of v3, /device:TPU:0, one launch (start us, length us, event | category | flops | bytes accessed | tf_op | source)
XLA Modules:
  0.0 158.2 jit_solution(14559133885108866163)
XLA Ops:
  7.2 1.8 %pad_maximum_fusion.1 = bf16[2,128,512]{2,1,0:T(8,128)(2,1)} fusion(bf16[1,128,512]{2,1,0:T(8,128)(2,1)} %bitcast.88, bf16[1,128,512]{2,1,0:T(8,128)(2,1)} %bitcast.89), kind=kLoop, calls=%fused_computation.1 | loop fusion | flops 131072 | bytes 524288 | tf_op jit(solution)/shard_map/stack | solution.py:235
  10.4 23.7 %all_to_all.10.refs_0_ = bf16[16,3,4,16,128]{4,3,2,1,0:T(8,128)(2,1)S(1)} all-to-all(bf16[16,3,4,16,128]{4,3,2,1,0:T(8,128)(2,1)S(1)} %pad_maximum_fusion), channel_id=1, replica_groups=mesh['y'=4,'c'=2,'x'=4,'z'=4] {'x','z'}, dimensions={0} | all-to-all | bytes 1572864 | tf_op jit(solution)/shard_map/all_to_all | solution.py:244
  35.1 3.1 %collective-permute-start.5 = (bf16[96,16,128]{2,1,0:T(8,128)(2,1)S(1)}, bf16[96,16,128]{2,1,0:T(8,128)(2,1)S(1)}, u32[]{:S(2)}, u32[]{:S(2)}) collective-permute-start(bf16[96,16,128]{2,1,0:T(8,128)(2,1)S(1)} %bitcast.83), channel_id=1, source_target_pairs={{0,96},{32,0},{64,32},{96,64},{1,97},{33,1},{65,33},{97,65},{2,98}... | collective-permute-start | bytes 1179656 | tf_op jit(solution)/shard_map/ppermute | solution.py:179
  38.2 3.2 %collective-permute-start.6 = (bf16[96,16,128]{2,1,0:T(8,128)(2,1)}, bf16[96,16,128]{2,1,0:T(8,128)(2,1)}, u32[]{:S(2)}, u32[]{:S(2)}) collective-permute-start(bf16[96,16,128]{2,1,0:T(8,128)(2,1)} %bitcast.19), channel_id=1, source_target_pairs={{0,96},{32,0},{64,32},{96,64},{1,97},{33,1},{65,33},{97,65},{2,98}... | collective-permute-start | bytes 1179656 | tf_op jit(solution)/shard_map/ppermute | solution.py:179
  41.4 6.3 %collective-permute-done.5.refs_6_ = bf16[96,16,128]{2,1,0:T(8,128)(2,1)S(1)} collective-permute-done((bf16[96,16,128]{2,1,0:T(8,128)(2,1)S(1)}, bf16[96,16,128]{2,1,0:T(8,128)(2,1)S(1)}, u32[]{:S(2)}, u32[]{:S(2)}) %collective-permute-start.5) | collective-permute-done | bytes 393248 | tf_op jit(solution)/shard_map/ppermute | solution.py:179
  47.7 3.8 %collective-permute-done.1.refs_2_ = bf16[96,16,128]{2,1,0:T(8,128)(2,1)} collective-permute-done((bf16[96,16,128]{2,1,0:T(8,128)(2,1)S(1)}, bf16[96,16,128]{2,1,0:T(8,128)(2,1)}, u32[]{:S(2)}, u32[]{:S(2)}) %collective-permute-start.1) | collective-permute-done | bytes 393248 | tf_op jit(solution)/shard_map/ppermute | solution.py:179
  52.5 3.7 %collective-permute-start.10 = (bf16[96,16,128]{2,1,0:T(8,128)(2,1)}, bf16[96,16,128]{2,1,0:T(8,128)(2,1)}, u32[]{:S(2)}, u32[]{:S(2)}) collective-permute-start(bf16[96,16,128]{2,1,0:T(8,128)(2,1)} %collective-permute-done.6.refs_7_), channel_id=1, source_target_pairs={{0,96},{32,0},{64,32},{96,64},{1,97},{33,1},{65,33},{97,65},{2,98}... | collective-permute-start | bytes 1179656 | tf_op jit(solution)/shard_map/ppermute | solution.py:179
  62.3 2.0 %collective-permute-done.9.refs_10_ = bf16[96,16,128]{2,1,0:T(8,128)(2,1)} collective-permute-done((bf16[96,16,128]{2,1,0:T(8,128)(2,1)}, bf16[96,16,128]{2,1,0:T(8,128)(2,1)}, u32[]{:S(2)}, u32[]{:S(2)}) %collective-permute-start.9) | collective-permute-done | bytes 393248 | tf_op jit(solution)/shard_map/ppermute | solution.py:179
  67.7 15.4 %owner.1 = (bf16[3,7,128,128]{3,2,1,0:T(8,128)(2,1)}, bf16[128,896]{1,0:T(8,128)(2,1)}, bf16[8,192,16,128]{3,2,1,0:T(8,128)(2,1)}, bf16[4,128,512]{2,1,0:T(8,128...) custom-call(s32[192]{0:T(256)} %get-tuple-element.29.rows, ...), custom_call_target="tpu_custom_call" | custom-call | tf_op jit(solution)/shard_map/owner/pallas_call | solution.py:271
  83.0 2.5 %collective-permute-start.13 = (bf16[4,128,512]{2,1,0:T(8,128)(2,1)}, bf16[4,128,512]{2,1,0:T(8,128)(2,1)S(1)}, u32[]{:S(2)}, u32[]{:S(2)}) collective-permute-start(bf16[4,128,512]{2,1,0:T(8,128)(2,1)} %get-tuple-element.19), channel_id=1, source_target_pairs={{0,12},{4,0},{8,4},{12,8},{1,13},{5,1},{9,5},{13,9},{2,14},{6,2},{... | collective-permute-start | bytes 1572872 | tf_op jit(solution)/shard_map/ppermute | solution.py:179
  86.7 7.6 %shard_map.136 = (bf16[4,128,512]{2,1,0:T(8,128)(2,1)}, bf16[4,128,512]{2,1,0:T(8,128)(2,1)}, bf16[4,128,512]{2,1,0:T(8,128)(2,1)}, bf16[4,128,512]{2,1,0:T(8,128)(2,1)}) custom-call(s32[192]{0:T(256)} %get-tuple-element.28.hops.rows, s32[192]{0:T(256)} %select_reduce_fusion.cols, s32[8]{0:T(128)} %stack.63.slots, ...), custom_call_target="tpu_custom_call" | custom-call | tf_op jit(solution)/shard_map/pallas_call | solution.py:297
  96.7 12.1 %collective-permute-done.13 = bf16[4,128,512]{2,1,0:T(8,128)(2,1)S(1)} collective-permute-done((bf16[4,128,512]{2,1,0:T(8,128)(2,1)}, bf16[4,128,512]{2,1,0:T(8,128)(2,1)S(1)}, u32[]{:S(2)}, u32[]{:S(2)}) %collective-permute-start.13) | collective-permute-done | bytes 524320 | tf_op jit(solution)/shard_map/ppermute | solution.py:179
  109.4 3.0 %collective-permute-done.15 = bf16[4,128,512]{2,1,0:T(8,128)(2,1)} collective-permute-done((bf16[4,128,512]{2,1,0:T(8,128)(2,1)}, bf16[4,128,512]{2,1,0:T(8,128)(2,1)}, u32[]{:S(2)}, u32[]{:S(2)}) %collective-permute-start.15) | collective-permute-done | bytes 524320 | tf_op jit(solution)/shard_map/ppermute | solution.py:179
  112.4 2.1 %fusion.6 = (bf16[128,512]{1,0:T(8,128)(2,1)}, bf16[128,512]{1,0:T(8,128)(2,1)}, bf16[128,512]{1,0:T(8,128)(2,1)S(1)}) fusion(bf16[4,128,512]{2,1,0:T(8,128)(2,1)} %collective-permute-done.15, bf16[4,128,512]{2,1,0:T(8,128)(2,1)} %collective-permute-done.14, bf16[4,128,512]{2,1,0:T(8,128)(2,1)S(1)} %collective-permute-done.13, ...), kind=kLoop, calls=%fused_computation.18 | loop fusion | flops 1572864 | bytes 1966080 | tf_op jit(solution)/shard_map/add | solution.py:183
  114.8 1.7 %collective-permute-start.18 = (bf16[128,512]{1,0:T(8,128)(2,1)}, bf16[128,512]{1,0:T(8,128)(2,1)S(1)}, u32[]{:S(2)}, u32[]{:S(2)}) collective-permute-start(bf16[128,512]{1,0:T(8,128)(2,1)} %get-tuple-element.34), channel_id=1, source_target_pairs={{0,1},{1,2},{2,3},{3,0},{4,5},{5,6},{6,7},{7,4},{8,9},{9,10},{10,1... | collective-permute-start | bytes 393224 | tf_op jit(solution)/shard_map/ppermute | solution.py:179
  116.6 8.6 %reduce-scatter.2.cloned.1.call-done = bf16[1,192,16,128]{3,2,1,0:T(8,128)(2,1)} async-done(((bf16[8,192,16,128]{3,2,1,0:T(8,128)(2,1)}), bf16[1,192,16,128]{3,2,1,0:T(8,128)(2,1)}) %reduce-scatter.2.cloned.1.call-update) | async-done | bytes 786448 | tf_op jit(solution)/shard_map/reduce_scatter | solution.py:292
  125.2 6.8 %all-to-all-start.1 = ((bf16[16,3,4,16,128]{4,3,2,1,0:T(8,128)(2,1)}), bf16[16,3,4,16,128]{4,3,2,1,0:T(8,128)(2,1)S(1)}, u32[]{:S(2)}, u32[]{:S(2)}) async-start(bf16[16,3,4,16,128]{4,3,2,1,0:T(8,128)(2,1)} %bitcast.82), calls=%async_computation.2 | async-start | bytes 1572864 | tf_op jit(solution)/shard_map/all_to_all | solution.py:313
  132.0 3.5 %collective-permute-start.17 = (bf16[128,512]{1,0:T(8,128)(2,1)S(1)}, bf16[128,512]{1,0:T(8,128)(2,1)S(1)}, u32[]{:S(2)}, u32[]{:S(2)}) collective-permute-start(bf16[128,512]{1,0:T(8,128)(2,1)S(1)} %get-tuple-element.35), channel_id=1, source_target_pairs={{0,2},{1,3},{2,0},{3,1},{4,6},{5,7},{6,4},{7,5},{8,10},{9,11},{10,... | collective-permute-start | bytes 393224 | tf_op jit(solution)/shard_map/ppermute | solution.py:179
  135.5 1.6 %fusion.9 = (bf16[128,512]{1,0:T(8,128)(2,1)S(1)}, bf16[128,512]{1,0:T(8,128)(2,1)S(1)}, bf16[128,512]{1,0:T(8,128)(2,1)S(1)}) fusion(bf16[4,128,512]{2,1,0:T(8,128)(2,1)} %collective-permute-done.21, bf16[4,128,512]{2,1,0:T(8,128)(2,1)} %collective-permute-done.20, bf16[4,128,512]{2,1,0:T(8,128)(2,1)} %collective-permute-done.19, ...), kind=kLoop, calls=%fused_computation.21 | loop fusion | flops 1572864 | bytes 1966080 | tf_op jit(solution)/shard_map/add | solution.py:183
  137.1 2.7 %collective-permute-start.22 = (bf16[128,512]{1,0:T(8,128)(2,1)S(1)}, bf16[128,512]{1,0:T(8,128)(2,1)S(1)}, u32[]{:S(2)}, u32[]{:S(2)}) collective-permute-start(bf16[128,512]{1,0:T(8,128)(2,1)S(1)} %get-tuple-element.30), channel_id=1, source_target_pairs={{0,12},{4,0},{8,4},{12,8},{1,13},{5,1},{9,5},{13,9},{2,14},{6,2},{... | collective-permute-start | bytes 393224 | tf_op jit(solution)/shard_map/ppermute | solution.py:179
  139.9 2.3 %collective-permute-start.23 = (bf16[128,512]{1,0:T(8,128)(2,1)S(1)}, bf16[128,512]{1,0:T(8,128)(2,1)S(1)}, u32[]{:S(2)}, u32[]{:S(2)}) collective-permute-start(bf16[128,512]{1,0:T(8,128)(2,1)S(1)} %get-tuple-element.32), channel_id=1, source_target_pairs={{0,8},{4,12},{8,0},{12,4},{1,9},{5,13},{9,1},{13,5},{2,10},{6,14},... | collective-permute-start | bytes 393224 | tf_op jit(solution)/shard_map/ppermute | solution.py:179
  142.2 2.1 %collective-permute-done.17 = bf16[128,512]{1,0:T(8,128)(2,1)S(1)} collective-permute-done((bf16[128,512]{1,0:T(8,128)(2,1)S(1)}, bf16[128,512]{1,0:T(8,128)(2,1)S(1)}, u32[]{:S(2)}, u32[]{:S(2)}) %collective-permute-start.17) | collective-permute-done | bytes 131104 | tf_op jit(solution)/shard_map/ppermute | solution.py:179
  144.3 1.9 %fusion.5 = bf16[128,512]{1,0:T(8,128)(2,1)} fusion(bf16[128,512]{1,0:T(8,128)(2,1)S(1)} %collective-permute-done.18, bf16[128,512]{1,0:T(8,128)(2,1)S(1)} %collective-permute-done.17, bf16[128,512]{1,0:T(8,128)(2,1)S(1)} %collective-permute-done.16, bf16[4,128,512]{2,1,0:T(8,128)(2,1)} %collective-permute-done.15, ...), kind=kLoop, calls=%fused_computation.9 | loop fusion | flops 917504 | bytes 1048576 | tf_op jit(solution)/shard_map/convert_element_type | solution.py:207
  148.6 1.9 %fusion.2 = bf16[128,512]{1,0:T(8,128)(2,1)} fusion(bf16[128,512]{1,0:T(8,128)(2,1)S(1)} %collective-permute-done.24, bf16[128,512]{1,0:T(8,128)(2,1)S(1)} %collective-permute-done.23, bf16[128,512]{1,0:T(8,128)(2,1)S(1)} %collective-permute-done.22, bf16[4,128,512]{2,1,0:T(8,128)(2,1)} %collective-permute-done.21, ...), kind=kLoop, calls=%fused_computation.5 | loop fusion | flops 917504 | bytes 1048576 | tf_op jit(solution)/shard_map/convert_element_type | solution.py:207
  (83 shorter events, 20.4 us)
Async XLA Ops:
  7.2 60.5 %all-gather.3.cloned.1.call-start = ((), (), s32[]{:S(2)}) async-start(), calls=%async_computation.4 | async-start | bytes 4456448 | tf_op jit(solution)/shard_map/all_gather | solution.py:235
  9.1 116.1 %reduce-scatter.2.cloned.1.call-start = ((), (), s32[]{:S(2)}) async-start(), calls=%async_computation.3 | async-start | bytes 7077888 | tf_op jit(solution)/shard_map/reduce_scatter | solution.py:292
  35.1 12.6 %collective-permute-start.5 = (bf16[96,16,128]{2,1,0:T(8,128)(2,1)S(1)}, bf16[96,16,128]{2,1,0:T(8,128)(2,1)S(1)}, u32[]{:S(2)}, u32[]{:S(2)}) collective-permute-start(bf16[96,16,128]{2,1,0:T(8,128)(2,1)S(1)} %bitcast.83), channel_id=1, source_target_pairs={{0,96},{32,0},{64,32},{96,64},{1,97},{33,1},{65,33},{97,65},{2,98}... | collective-permute-start | bytes 1179656 | tf_op jit(solution)/shard_map/ppermute | solution.py:179
  38.2 13.3 %collective-permute-start.1 = (bf16[96,16,128]{2,1,0:T(8,128)(2,1)S(1)}, bf16[96,16,128]{2,1,0:T(8,128)(2,1)}, u32[]{:S(2)}, u32[]{:S(2)}) collective-permute-start(bf16[96,16,128]{2,1,0:T(8,128)(2,1)S(1)} %bitcast.84), channel_id=1, source_target_pairs={{0,32},{32,64},{64,96},{96,0},{1,33},{33,65},{65,97},{97,1},{2,34}... | collective-permute-start | bytes 1179656 | tf_op jit(solution)/shard_map/ppermute | solution.py:179
  38.2 14.3 %collective-permute-start.6 = (bf16[96,16,128]{2,1,0:T(8,128)(2,1)}, bf16[96,16,128]{2,1,0:T(8,128)(2,1)}, u32[]{:S(2)}, u32[]{:S(2)}) collective-permute-start(bf16[96,16,128]{2,1,0:T(8,128)(2,1)} %bitcast.19), channel_id=1, source_target_pairs={{0,96},{32,0},{64,32},{96,64},{1,97},{33,1},{65,33},{97,65},{2,98}... | collective-permute-start | bytes 1179656 | tf_op jit(solution)/shard_map/ppermute | solution.py:179
  41.4 19.1 %collective-permute-start.2 = (bf16[96,16,128]{2,1,0:T(8,128)(2,1)}, bf16[96,16,128]{2,1,0:T(8,128)(2,1)}, u32[]{:S(2)}, u32[]{:S(2)}) collective-permute-start(bf16[96,16,128]{2,1,0:T(8,128)(2,1)} %bitcast.19), channel_id=1, source_target_pairs={{0,32},{32,64},{64,96},{96,0},{1,33},{33,65},{65,97},{97,1},{2,34}... | collective-permute-start | bytes 1179656 | tf_op jit(solution)/shard_map/ppermute | solution.py:179
  47.7 14.0 %collective-permute-start.7 = (bf16[96,16,128]{2,1,0:T(8,128)(2,1)S(1)}, bf16[96,16,128]{2,1,0:T(8,128)(2,1)}, u32[]{:S(2)}, u32[]{:S(2)}) collective-permute-start(bf16[96,16,128]{2,1,0:T(8,128)(2,1)S(1)} %collective-permute-done.5.refs_6_), channel_id=1, source_target_pairs={{0,16},{16,0},{1,17},{17,1},{2,18},{18,2},{3,19},{19,3},{4,20},{20... | collective-permute-start | bytes 1179656 | tf_op jit(solution)/shard_map/ppermute | solution.py:179
  51.5 12.8 %collective-permute-start.9 = (bf16[96,16,128]{2,1,0:T(8,128)(2,1)}, bf16[96,16,128]{2,1,0:T(8,128)(2,1)}, u32[]{:S(2)}, u32[]{:S(2)}) collective-permute-start(bf16[96,16,128]{2,1,0:T(8,128)(2,1)} %collective-permute-done.1.refs_2_), channel_id=1, source_target_pairs={{0,32},{32,64},{64,96},{96,0},{1,33},{33,65},{65,97},{97,1},{2,34}... | collective-permute-start | bytes 1179656 | tf_op jit(solution)/shard_map/ppermute | solution.py:179
  51.5 12.9 %collective-permute-start.3 = (bf16[96,16,128]{2,1,0:T(8,128)(2,1)}, bf16[96,16,128]{2,1,0:T(8,128)(2,1)}, u32[]{:S(2)}, u32[]{:S(2)}) collective-permute-start(bf16[96,16,128]{2,1,0:T(8,128)(2,1)} %collective-permute-done.1.refs_2_), channel_id=1, source_target_pairs={{0,16},{16,0},{1,17},{17,1},{2,18},{18,2},{3,19},{19,3},{4,20},{20... | collective-permute-start | bytes 1179656 | tf_op jit(solution)/shard_map/ppermute | solution.py:179
  52.5 12.4 %collective-permute-start.10 = (bf16[96,16,128]{2,1,0:T(8,128)(2,1)}, bf16[96,16,128]{2,1,0:T(8,128)(2,1)}, u32[]{:S(2)}, u32[]{:S(2)}) collective-permute-start(bf16[96,16,128]{2,1,0:T(8,128)(2,1)} %collective-permute-done.6.refs_7_), channel_id=1, source_target_pairs={{0,96},{32,0},{64,32},{96,64},{1,97},{33,1},{65,33},{97,65},{2,98}... | collective-permute-start | bytes 1179656 | tf_op jit(solution)/shard_map/ppermute | solution.py:179
  60.5 7.1 %collective-permute-start = (bf16[192,16,128]{2,1,0:T(8,128)(2,1)S(1)}, bf16[192,16,128]{2,1,0:T(8,128)(2,1)}, u32[]{:S(2)}, u32[]{:S(2)}) collective-permute-start(bf16[192,16,128]{2,1,0:T(8,128)(2,1)S(1)} %bitcast.75), channel_id=1, source_target_pairs={{0,16},{16,0},{1,17},{17,1},{2,18},{18,2},{3,19},{19,3},{4,20},{20... | collective-permute-start | bytes 2359304 | tf_op jit(solution)/shard_map/ppermute | solution.py:179
  83.0 25.8 %collective-permute-start.13 = (bf16[4,128,512]{2,1,0:T(8,128)(2,1)}, bf16[4,128,512]{2,1,0:T(8,128)(2,1)S(1)}, u32[]{:S(2)}, u32[]{:S(2)}) collective-permute-start(bf16[4,128,512]{2,1,0:T(8,128)(2,1)} %get-tuple-element.19), channel_id=1, source_target_pairs={{0,12},{4,0},{8,4},{12,8},{1,13},{5,1},{9,5},{13,9},{2,14},{6,2},{... | collective-permute-start | bytes 1572872 | tf_op jit(solution)/shard_map/ppermute | solution.py:179
  85.5 23.9 %collective-permute-start.14 = (bf16[4,128,512]{2,1,0:T(8,128)(2,1)}, bf16[4,128,512]{2,1,0:T(8,128)(2,1)}, u32[]{:S(2)}, u32[]{:S(2)}) collective-permute-start(bf16[4,128,512]{2,1,0:T(8,128)(2,1)} %get-tuple-element.20), channel_id=1, source_target_pairs={{0,8},{4,12},{8,0},{12,4},{1,9},{5,13},{9,1},{13,5},{2,10},{6,14},... | collective-permute-start | bytes 1572872 | tf_op jit(solution)/shard_map/ppermute | solution.py:179
  85.9 26.5 %collective-permute-start.15 = (bf16[4,128,512]{2,1,0:T(8,128)(2,1)}, bf16[4,128,512]{2,1,0:T(8,128)(2,1)}, u32[]{:S(2)}, u32[]{:S(2)}) collective-permute-start(bf16[4,128,512]{2,1,0:T(8,128)(2,1)} %get-tuple-element.21), channel_id=1, source_target_pairs={{0,4},{4,8},{8,12},{12,0},{1,5},{5,9},{9,13},{13,1},{2,6},{6,10},{... | collective-permute-start | bytes 1572872 | tf_op jit(solution)/shard_map/ppermute | solution.py:179
  94.3 37.6 %collective-permute-start.19 = (bf16[4,128,512]{2,1,0:T(8,128)(2,1)}, bf16[4,128,512]{2,1,0:T(8,128)(2,1)}, u32[]{:S(2)}, u32[]{:S(2)}) collective-permute-start(bf16[4,128,512]{2,1,0:T(8,128)(2,1)} %get-tuple-element.24), channel_id=1, source_target_pairs={{0,3},{1,0},{2,1},{3,2},{4,7},{5,4},{6,5},{7,6},{8,11},{9,8},{10,9... | collective-permute-start | bytes 1572872 | tf_op jit(solution)/shard_map/ppermute | solution.py:179
  95.8 39.7 %collective-permute-start.20 = (bf16[4,128,512]{2,1,0:T(8,128)(2,1)}, bf16[4,128,512]{2,1,0:T(8,128)(2,1)}, u32[]{:S(2)}, u32[]{:S(2)}) collective-permute-start(bf16[4,128,512]{2,1,0:T(8,128)(2,1)} %get-tuple-element.25), channel_id=1, source_target_pairs={{0,2},{1,3},{2,0},{3,1},{4,6},{5,7},{6,4},{7,5},{8,10},{9,11},{10,... | collective-permute-start | bytes 1572872 | tf_op jit(solution)/shard_map/ppermute | solution.py:179
  108.9 26.6 %collective-permute-start.21 = (bf16[4,128,512]{2,1,0:T(8,128)(2,1)}, bf16[4,128,512]{2,1,0:T(8,128)(2,1)}, u32[]{:S(2)}, u32[]{:S(2)}) collective-permute-start(bf16[4,128,512]{2,1,0:T(8,128)(2,1)} %get-tuple-element.26), channel_id=1, source_target_pairs={{0,1},{1,2},{2,3},{3,0},{4,5},{5,6},{6,7},{7,4},{8,9},{9,10},{10,1... | collective-permute-start | bytes 1572872 | tf_op jit(solution)/shard_map/ppermute | solution.py:179
  114.5 25.3 %collective-permute-start.16 = (bf16[128,512]{1,0:T(8,128)(2,1)}, bf16[128,512]{1,0:T(8,128)(2,1)S(1)}, u32[]{:S(2)}, u32[]{:S(2)}) collective-permute-start(bf16[128,512]{1,0:T(8,128)(2,1)} %get-tuple-element.33), channel_id=1, source_target_pairs={{0,3},{1,0},{2,1},{3,2},{4,7},{5,4},{6,5},{7,6},{8,11},{9,8},{10,9... | collective-permute-start | bytes 393224 | tf_op jit(solution)/shard_map/ppermute | solution.py:179
  114.8 27.4 %collective-permute-start.18 = (bf16[128,512]{1,0:T(8,128)(2,1)}, bf16[128,512]{1,0:T(8,128)(2,1)S(1)}, u32[]{:S(2)}, u32[]{:S(2)}) collective-permute-start(bf16[128,512]{1,0:T(8,128)(2,1)} %get-tuple-element.34), channel_id=1, source_target_pairs={{0,1},{1,2},{2,3},{3,0},{4,5},{5,6},{6,7},{7,4},{8,9},{9,10},{10,1... | collective-permute-start | bytes 393224 | tf_op jit(solution)/shard_map/ppermute | solution.py:179
  125.2 25.3 %all-to-all-start.1 = ((bf16[16,3,4,16,128]{4,3,2,1,0:T(8,128)(2,1)}), bf16[16,3,4,16,128]{4,3,2,1,0:T(8,128)(2,1)S(1)}, u32[]{:S(2)}, u32[]{:S(2)}) async-start(bf16[16,3,4,16,128]{4,3,2,1,0:T(8,128)(2,1)} %bitcast.82), calls=%async_computation.2 | async-start | bytes 1572864 | tf_op jit(solution)/shard_map/all_to_all | solution.py:313
  132.0 12.4 %collective-permute-start.17 = (bf16[128,512]{1,0:T(8,128)(2,1)S(1)}, bf16[128,512]{1,0:T(8,128)(2,1)S(1)}, u32[]{:S(2)}, u32[]{:S(2)}) collective-permute-start(bf16[128,512]{1,0:T(8,128)(2,1)S(1)} %get-tuple-element.35), channel_id=1, source_target_pairs={{0,2},{1,3},{2,0},{3,1},{4,6},{5,7},{6,4},{7,5},{8,10},{9,11},{10,... | collective-permute-start | bytes 393224 | tf_op jit(solution)/shard_map/ppermute | solution.py:179
  137.1 9.1 %collective-permute-start.22 = (bf16[128,512]{1,0:T(8,128)(2,1)S(1)}, bf16[128,512]{1,0:T(8,128)(2,1)S(1)}, u32[]{:S(2)}, u32[]{:S(2)}) collective-permute-start(bf16[128,512]{1,0:T(8,128)(2,1)S(1)} %get-tuple-element.30), channel_id=1, source_target_pairs={{0,12},{4,0},{8,4},{12,8},{1,13},{5,1},{9,5},{13,9},{2,14},{6,2},{... | collective-permute-start | bytes 393224 | tf_op jit(solution)/shard_map/ppermute | solution.py:179
  139.9 7.3 %collective-permute-start.24 = (bf16[128,512]{1,0:T(8,128)(2,1)S(1)}, bf16[128,512]{1,0:T(8,128)(2,1)S(1)}, u32[]{:S(2)}, u32[]{:S(2)}) collective-permute-start(bf16[128,512]{1,0:T(8,128)(2,1)S(1)} %get-tuple-element.31), channel_id=1, source_target_pairs={{0,4},{4,8},{8,12},{12,0},{1,5},{5,9},{9,13},{13,1},{2,6},{6,10},{... | collective-permute-start | bytes 393224 | tf_op jit(solution)/shard_map/ppermute | solution.py:179
  139.9 8.7 %collective-permute-start.23 = (bf16[128,512]{1,0:T(8,128)(2,1)S(1)}, bf16[128,512]{1,0:T(8,128)(2,1)S(1)}, u32[]{:S(2)}, u32[]{:S(2)}) collective-permute-start(bf16[128,512]{1,0:T(8,128)(2,1)S(1)} %get-tuple-element.32), channel_id=1, source_target_pairs={{0,8},{4,12},{8,0},{12,4},{1,9},{5,13},{9,1},{13,5},{2,10},{6,14},... | collective-permute-start | bytes 393224 | tf_op jit(solution)/shard_map/ppermute | solution.py:179
  (12 other events, 212.2 us)
Sparse Core Ops, SparseCore 0:
  10.7 55.9 all-gather.2
  83.2 41.9 reduce-scatter.1
